TPU v7x, 32 devices: a whole 2x2x4 slice. The times are simulated.
32 devices in a mesh: batch: 4 (over y, x), filt: 8 (over z, core).
Axes of the slice: x: 2, y: 2, z: 4, core: 2. Of those that a mesh axis runs over, the one named last changes fastest.
Arguments:
- images: bfloat16 [768, 3072], P(('batch', 'filt')), may hold values from -6 to 6
- labels: int32 [768], P(('batch', 'filt')), may hold values from 0 to 9
- partner: int32 [768], P(('batch', 'filt')), may hold values from 0 to 767, as said below
- valid_mask: int32 [768], P(('batch', 'filt')), may hold values from 0 to 1, as said below
- group_sizes: int32 [4, 8], replicated, may hold values from 1 to 185, as said below
- stem_weight: float32 [16, 27], replicated, may hold values from -1.25 to 1.25
- bridge_weight: float32 [640, 16], P('filt'), may hold values from -1.5 to 1.5
- conv_weight: float32 [2, 640, 9, 640], P(None, 'filt'), may hold values from -0.078125 to 0.078125
- norm_params: float32 [6, 640], P(None, 'filt'), may hold values from 0.5 to 1.5
- head_weight: float32 [10, 640], P(None, 'filt'), may hold values from -1 to 1
- head_bias: float32 [10], replicated, may hold values from -3 to 3
- stem_first: float32 [16, 27], replicated, may hold values from -4.7683716e-06 to 4.7683716e-06
- stem_second: float32 [16, 27], replicated, may hold values from 1.2540817e-12 to 2.002716e-11
- bridge_first: float32 [640, 16], P('filt'), may hold values from -9.536743e-07 to 9.536743e-07
- bridge_second: float32 [640, 16], P('filt'), may hold values from 5.016327e-14 to 8.010864e-13
- conv_first: float32 [2, 640, 9, 640], P(None, 'filt'), may hold values from -2.3841858e-06 to 2.3841858e-06
- conv_second: float32 [2, 640, 9, 640], P(None, 'filt'), may hold values from 3.5671658e-13 to 5.6966146e-12
- norm_first: float32 [6, 640], P(None, 'filt'), may hold values from -7.6293945e-06 to 7.6293945e-06
- norm_second: float32 [6, 640], P(None, 'filt'), may hold values from 3.2104493e-12 to 5.126953e-11
- head_first: float32 [10, 640], P(None, 'filt'), may hold values from -7.6293945e-06 to 7.6293945e-06
- head_second: float32 [10, 640], P(None, 'filt'), may hold values from 3.2104493e-12 to 5.126953e-11
- bias_first: float32 [10], replicated, may hold values from -2.2888184e-05 to 2.2888184e-05
- bias_second: float32 [10], replicated, may hold values from 3.5671657e-11 to 5.696615e-10
Outputs:
- stem_weight_new: float32 [16, 27], replicated
- stem_first_new: float32 [16, 27], replicated
- stem_second_new: float32 [16, 27], replicated
- bridge_weight_new: float32 [640, 16], P('filt')
- bridge_first_new: float32 [640, 16], P('filt')
- bridge_second_new: float32 [640, 16], P('filt')
- conv_weight_new: float32 [2, 640, 9, 640], P(None, 'filt')
- conv_first_new: float32 [2, 640, 9, 640], P(None, 'filt')
- conv_second_new: float32 [2, 640, 9, 640], P(None, 'filt')
- norm_params_new: float32 [6, 640], P(None, 'filt')
- norm_first_new: float32 [6, 640], P(None, 'filt')
- norm_second_new: float32 [6, 640], P(None, 'filt')
- head_weight_new: float32 [10, 640], P(None, 'filt')
- head_first_new: float32 [10, 640], P(None, 'filt')
- head_second_new: float32 [10, 640], P(None, 'filt')
- head_bias_new: float32 [10], replicated
- bias_first_new: float32 [10], replicated
- bias_second_new: float32 [10], replicated
- grad_norm: float32 [], replicated
- loss: float32 [], replicated
Inputs may be any that keep to these rules, and one draw needn't show every extreme that they name: `group_sizes`: row b lists the sizes of the 8 groups of batch shard b, laid one after another from the shard's first slot; a shard's sizes sum to at most 192, and in one shard exactly. `valid_mask`: slots after a shard's groups hold 0; the first slot of every group holds 1, and so does image 768 - 1. `partner`: each entry is the index of an image whose valid_mask is 1.
All inputs are finite; a program needn't handle non-finite values.
Results may differ from a plain program's by a relative error of at most 0.008.
The roundings to bfloat16 on the way count: a program that leaves them out, or rounds other values in their place, can miss the bound.
Values may be sent and summed in bfloat16 or wider, within the bound.
A program may use at most 256 MiB of HBM per device.

v0:
```python
import jax
import jax.numpy as jnp
from jax import lax
from jax.sharding import PartitionSpec as P

STEP = 8


beta_one = 0.9
beta_two = 0.95
adam_eps = 1e-08
norm_epsilon = 1e-05
clip_norm = 0.01
own_share = 0.7


def make_patches(images):
    number = images.shape[0]
    grid = images.reshape(number, 3, 32, 32)
    padded = jnp.pad(grid, ((0, 0), (0, 0), (1, 1), (1, 1)))
    pieces = [
        padded[:, :, row_off : row_off + 29 : 4, col_off : col_off + 29 : 4]
        for row_off in range(3)
        for col_off in range(3)
    ]
    stacked = jnp.stack(pieces, axis=2)
    return jnp.transpose(stacked, (1, 2, 0, 3, 4)).reshape(27, number * 64)


def shifted(feature_field):
    width, rows = feature_field.shape
    grid = feature_field.reshape(width, rows // 64, 8, 8)
    padded = jnp.pad(grid, ((0, 0), (0, 0), (1, 1), (1, 1)))
    pieces = [
        padded[:, :, row_off : row_off + 8, col_off : col_off + 8]
        for row_off in range(3)
        for col_off in range(3)
    ]
    return jnp.stack(pieces, axis=0).reshape(9 * width, rows)


def unshifted(parts, width):
    rows = parts.shape[1]
    grid = parts.reshape(9, width, rows // 64, 8, 8)
    summed = jnp.zeros((width, rows // 64, 10, 10), jnp.float32)
    for row_off in range(3):
        for col_off in range(3):
            summed = summed + jnp.pad(
                grid[3 * row_off + col_off],
                ((0, 0), (0, 0), (row_off, 2 - row_off), (col_off, 2 - col_off)),
            )
    return summed[:, :, 1:9, 1:9].reshape(width, rows)


def image_weights(valid_mask, group_sizes):
    shards, groups = group_sizes.shape
    capacity = valid_mask.shape[0] // shards
    group_ends = jnp.cumsum(group_sizes, axis=1)
    slot_index = jnp.arange(capacity, dtype=jnp.int32)
    member = jnp.sum(
        (slot_index[None, :, None] >= group_ends[:, None, :]).astype(jnp.int32), axis=2
    )
    member = jnp.minimum(member, groups - 1)
    chosen = (member[:, :, None] == jnp.arange(groups, dtype=jnp.int32)[None, None, :]).astype(
        jnp.float32
    )
    sizes_each = jnp.sum(chosen * group_sizes[:, None, :].astype(jnp.float32), axis=2)
    return valid_mask.astype(jnp.float32) / sizes_each.reshape(-1)


def norm_forward(feature_field, norm_gain, norm_shift, row_validity_mask, valid_count):
    batch_mean = (
        lax.psum(jnp.sum(feature_field * row_validity_mask, axis=1), ("batch", "filt"))
        / valid_count
    )
    centered_input = feature_field - batch_mean[:, None]
    batch_variance = (
        lax.psum(
            jnp.sum(centered_input * centered_input * row_validity_mask, axis=1), ("batch", "filt")
        )
        / valid_count
    )
    inverse_scale = lax.rsqrt(batch_variance + norm_epsilon)
    normalized_input = (feature_field - batch_mean[:, None]) * inverse_scale[:, None]
    norm_output = jnp.maximum(norm_gain[:, None] * normalized_input + norm_shift[:, None], 0.0)
    return (norm_output, normalized_input, inverse_scale)


def masked_norm_backward(
    output_gradient,
    norm_output,
    normalized_input,
    inverse_scale,
    norm_gain,
    row_validity_mask,
    valid_count,
):
    passed_rows = jnp.where(norm_output > 0.0, output_gradient, 0.0)
    shift_gradient, gain_gradient = lax.psum(
        (jnp.sum(passed_rows, axis=1), jnp.sum(passed_rows * normalized_input, axis=1)),
        ("batch", "filt"),
    )
    input_gradient = (
        passed_rows
        - row_validity_mask[None, :]
        * (shift_gradient[:, None] + normalized_input * gain_gradient[:, None])
        / valid_count
    )
    return ((norm_gain * inverse_scale)[:, None] * input_gradient, gain_gradient, shift_gradient)


def conv_forward(feature_field, weight_shard):
    stacked = shifted(feature_field)
    low_shard = weight_shard.astype(jnp.bfloat16)
    piece = lax.all_gather(low_shard, "filt", axis=0, tiled=True)
    norm_output = jnp.dot(
        piece.reshape(piece.shape[0], -1), stacked, preferred_element_type=jnp.float32
    )
    return (norm_output, None)


def conv_backward(feature_field, weight_shard, output_gradient):
    width = feature_field.shape[0]
    stacked = shifted(feature_field)
    rows_grad = output_gradient
    term = lax.dot_general(
        rows_grad, stacked, (((1,), (1,)), ((), ())), preferred_element_type=jnp.float32
    )
    weight_grad = lax.psum_scatter(
        term.reshape(lax.axis_size("filt") * weight_shard.shape[0], 9, width),
        "filt",
        scatter_dimension=0,
        tiled=True,
    )
    piece = lax.all_gather(weight_shard.astype(jnp.bfloat16), "filt", axis=0, tiled=True)
    rows_grad = output_gradient
    back = lax.dot_general(
        piece.reshape(piece.shape[0], -1),
        rows_grad,
        (((0,), (0,)), ((), ())),
        preferred_element_type=jnp.float32,
    )
    return (unshifted(back, width), weight_grad)


def adam_step(weight, output_gradient, first, second, rate, shrink, factor):
    clipped = output_gradient * factor
    first = beta_one * first + (1.0 - beta_one) * clipped
    second = beta_two * second + (1.0 - beta_two) * clipped * clipped
    ahead = first / (1.0 - beta_one**STEP)
    behind = second / (1.0 - beta_two**STEP)
    return (
        weight - rate * (ahead / (jnp.sqrt(behind) + adam_eps) + shrink * weight),
        first,
        second,
    )


def body(
    images,
    labels,
    partner,
    valid_mask,
    group_sizes,
    stem_weight,
    bridge_weight,
    conv_weight,
    norm_params,
    head_weight,
    head_bias,
    stem_first,
    stem_second,
    bridge_first,
    bridge_second,
    conv_first,
    conv_second,
    norm_first,
    norm_second,
    head_first,
    head_second,
    bias_first,
    bias_second,
):
    width = bridge_weight.shape[0]
    bridge_all, norm_all, head_all = (
        lax.all_gather(bridge_weight, "filt", axis=0, tiled=True),
        lax.all_gather(norm_params, "filt", axis=1, tiled=True),
        lax.all_gather(head_weight, "filt", axis=1, tiled=True),
    )
    labels_all, valid_all = (
        lax.all_gather(labels, ("batch", "filt"), axis=0, tiled=True),
        lax.all_gather(valid_mask, ("batch", "filt"), axis=0, tiled=True),
    )
    weight_all = image_weights(valid_all, group_sizes)
    total = jnp.sum(weight_all)
    valid_count = 64.0 * jnp.sum(valid_all.astype(jnp.float32))
    local = images.shape[0]
    image_weight = lax.dynamic_slice_in_dim(
        weight_all, lax.axis_index(("batch", "filt")) * local, local
    )
    row_validity_mask = jnp.repeat(valid_mask.astype(jnp.float32), 64)
    patch = make_patches(images)
    stem = jnp.dot(
        stem_weight.astype(jnp.bfloat16), patch, preferred_element_type=jnp.float32
    ).astype(jnp.bfloat16)
    base = jnp.dot(bridge_all.astype(jnp.bfloat16), stem, preferred_element_type=jnp.float32)
    first, first_hat, first_scale = norm_forward(
        base, norm_all[0], norm_all[1], row_validity_mask, valid_count
    )
    first_low = first.astype(jnp.bfloat16)
    inner, kept_zero = conv_forward(first_low, conv_weight[0])
    second, second_hat, second_scale = norm_forward(
        inner, norm_all[2], norm_all[3], row_validity_mask, valid_count
    )
    second_low = second.astype(jnp.bfloat16)
    branch, kept_one = conv_forward(second_low, conv_weight[1])
    final, final_hat, final_scale = norm_forward(
        base + branch, norm_all[4], norm_all[5], row_validity_mask, valid_count
    )
    pooled = jnp.mean(final.reshape(final.shape[0], local, 64), axis=2).astype(jnp.bfloat16)
    logits = (
        jnp.dot(head_all.astype(jnp.bfloat16), pooled, preferred_element_type=jnp.float32)
        + head_bias[:, None]
    )
    moved = logits - jnp.max(logits, axis=0, keepdims=True)
    logp = moved - jnp.log(jnp.sum(jnp.exp(moved), axis=0, keepdims=True))
    classes = jnp.arange(logits.shape[0], dtype=jnp.int32)
    partner_labels = jnp.take(labels_all, partner)
    target = own_share * (labels[None, :] == classes[:, None]).astype(jnp.float32) + (
        1.0 - own_share
    ) * (partner_labels[None, :] == classes[:, None]).astype(jnp.float32)
    loss_part = -jnp.sum(image_weight * jnp.sum(target * logp, axis=0))
    d_logits = ((jnp.exp(logp) - target) * (image_weight / total)[None, :]).astype(jnp.bfloat16)
    bias_grad = jnp.sum(d_logits.astype(jnp.float32), axis=1)
    head_grad = lax.dot_general(
        d_logits, pooled, (((1,), (1,)), ((), ())), preferred_element_type=jnp.float32
    )
    d_pooled = lax.dot_general(
        head_all.astype(jnp.bfloat16),
        d_logits,
        (((0,), (0,)), ((), ())),
        preferred_element_type=jnp.float32,
    )
    d_final = jnp.repeat(d_pooled / 64.0, 64, axis=1)
    d_block, gain_two, shift_two = masked_norm_backward(
        d_final, final, final_hat, final_scale, norm_all[4], row_validity_mask, valid_count
    )
    d_second, conv_grad_one = conv_backward(
        second_low, conv_weight[1], d_block.astype(jnp.bfloat16)
    )
    d_inner, gain_one, shift_one = masked_norm_backward(
        d_second, second, second_hat, second_scale, norm_all[2], row_validity_mask, valid_count
    )
    d_first, conv_grad_zero = conv_backward(first_low, conv_weight[0], d_inner.astype(jnp.bfloat16))
    d_lower, gain_zero, shift_zero = masked_norm_backward(
        d_first, first, first_hat, first_scale, norm_all[0], row_validity_mask, valid_count
    )
    d_base = (d_block + d_lower).astype(jnp.bfloat16)
    bridge_grad = lax.dot_general(
        d_base, stem, (((1,), (1,)), ((), ())), preferred_element_type=jnp.float32
    )
    d_stem = lax.dot_general(
        bridge_all.astype(jnp.bfloat16),
        d_base,
        (((0,), (0,)), ((), ())),
        preferred_element_type=jnp.float32,
    ).astype(jnp.bfloat16)
    stem_grad = lax.dot_general(
        d_stem, patch, (((1,), (1,)), ((), ())), preferred_element_type=jnp.float32
    )
    bridge_part, head_part = (
        lax.psum_scatter(bridge_grad, "filt", scatter_dimension=0, tiled=True),
        lax.psum_scatter(head_grad, "filt", scatter_dimension=1, tiled=True),
    )
    conv_grad, bridge_sum, head_sum = lax.psum(
        (jnp.stack([conv_grad_zero, conv_grad_one]), bridge_part, head_part), "batch"
    )
    stem_sum, bias_sum, loss_sum = lax.psum((stem_grad, bias_grad, loss_part), ("batch", "filt"))
    norm_full = jnp.stack([gain_zero, shift_zero, gain_one, shift_one, gain_two, shift_two])
    norm_grad = lax.dynamic_slice_in_dim(norm_full, lax.axis_index("filt") * width, width, 1)
    owned_square = (
        jnp.sum(conv_grad * conv_grad)
        + jnp.sum(bridge_sum * bridge_sum)
        + jnp.sum(norm_grad * norm_grad)
        + jnp.sum(head_sum * head_sum)
    )
    squares_all = (
        lax.psum(owned_square, "filt") + jnp.sum(stem_sum * stem_sum) + jnp.sum(bias_sum * bias_sum)
    )
    grad_norm = jnp.sqrt(squares_all)
    factor = clip_norm / jnp.maximum(grad_norm, clip_norm)
    stem_new = adam_step(stem_weight, stem_sum, stem_first, stem_second, 0.5, 0.05, factor)
    bridge_new = adam_step(
        bridge_weight, bridge_sum, bridge_first, bridge_second, 0.6, 0.05, factor
    )
    conv_new = adam_step(conv_weight, conv_grad, conv_first, conv_second, 0.033, 0.05, factor)
    norm_new = adam_step(norm_params, norm_grad, norm_first, norm_second, 0.5, 0.0, factor)
    head_new = adam_step(head_weight, head_sum, head_first, head_second, 0.1, 0.05, factor)
    bias_new = adam_step(head_bias, bias_sum, bias_first, bias_second, 0.5, 0.0, factor)
    return (
        stem_new[0],
        stem_new[1],
        stem_new[2],
        bridge_new[0],
        bridge_new[1],
        bridge_new[2],
        conv_new[0],
        conv_new[1],
        conv_new[2],
        norm_new[0],
        norm_new[1],
        norm_new[2],
        head_new[0],
        head_new[1],
        head_new[2],
        bias_new[0],
        bias_new[1],
        bias_new[2],
        grad_norm,
        loss_sum / total,
    )


def solution(mesh):
    in_specs = (
        P(("batch", "filt"), None),
        P(("batch", "filt")),
        P(("batch", "filt")),
        P(("batch", "filt")),
        P(),
        P(),
        P("filt", None),
        P(None, "filt", None, None),
        P(None, "filt"),
        P(None, "filt"),
        P(),
        P(),
        P(),
        P("filt", None),
        P("filt", None),
        P(None, "filt", None, None),
        P(None, "filt", None, None),
        P(None, "filt"),
        P(None, "filt"),
        P(None, "filt"),
        P(None, "filt"),
        P(),
        P(),
    )
    out_specs = (
        P(),
        P(),
        P(),
        P("filt", None),
        P("filt", None),
        P("filt", None),
        P(None, "filt", None, None),
        P(None, "filt", None, None),
        P(None, "filt", None, None),
        P(None, "filt"),
        P(None, "filt"),
        P(None, "filt"),
        P(None, "filt"),
        P(None, "filt"),
        P(None, "filt"),
        P(),
        P(),
        P(),
        P(),
        P(),
    )
    return jax.shard_map(body, mesh=mesh, in_specs=in_specs, out_specs=out_specs, check_vma=False)
```

profile of v0, /device:TPU:1, one launch (start us, length us, event | category | flops | bytes accessed | tf_op | source)
XLA Modules:
  0.0 1181.5 jit_solution(9924384892840319865)
XLA Ops:
  22.0 15.7 %all-gather.3 = bf16[8,80,16]{1,2,0:T(8,128)(2,1)S(1)} all-gather(bf16[1,80,16]{1,2,0:T(8,128)(2,1)S(1)} %bitcast_convert_fusion.1), channel_id=1, replica_groups=mesh['batch'=4,'filt'=8] {'filt'}, dimensions={0}, use_global_device_ids=true | all-gather | bytes 23040 | tf_op jit(solution)/shard_map/all_gather | solution.py:186
  38.3 14.2 %all-gather.2 = f32[8,80,6]{1,2,0:T(8,128)S(1)} all-gather(f32[1,80,6]{1,2,0:T(8,128)S(1)} %bitcast.381), channel_id=1, replica_groups=mesh['batch'=4,'filt'=8] {'filt'}, dimensions={0}, use_global_device_ids=true | all-gather | bytes 17280 | tf_op jit(solution)/shard_map/all_gather | solution.py:187
  53.2 41.5 %all-reduce.23 = (s32[768]{0:T(1024)S(1)}, s32[768]{0:T(1024)S(1)}) all-reduce(s32[768]{0:T(1024)S(1)} %dynamic-update-slice, s32[768]{0:T(1024)S(1)} %dynamic-update-slice.1), channel_id=1, replica_groups=mesh['batch'=4,'filt'=8] {'batch','filt'}, use_global_device_ids=true, to_apply=%add.21 | all-reduce | flops 1536 | bytes 12288
  98.6 44.4 %psum.133 = f32[640]{0:T(1024)S(1)} all-reduce(f32[640]{0:T(1024)S(1)} %get-tuple-element.111), channel_id=1, replica_groups=mesh['batch'=4,'filt'=8] {'batch','filt'}, use_global_device_ids=true, to_apply=%region_1.2 | all-reduce | flops 640 | bytes 5120 | tf_op jit(solution)/shard_map/psum | solution.py:73
  145.8 40.3 %psum.134 = f32[640]{0:T(1024)S(1)} all-reduce(f32[640]{0:T(1024)S(1)} %multiply_reduce_fusion.4), channel_id=1, replica_groups=mesh['batch'=4,'filt'=8] {'batch','filt'}, use_global_device_ids=true, to_apply=%region_4.5 | all-reduce | flops 640 | bytes 5120 | tf_op jit(solution)/shard_map/psum | solution.py:78
  201.4 16.1 %all-gather.4 = bf16[8,80,10]{1,2,0:T(8,128)(2,1)S(1)} all-gather(bf16[1,80,10]{1,2,0:T(8,128)(2,1)S(1)} %bitcast_convert_fusion), channel_id=1, replica_groups=mesh['batch'=4,'filt'=8] {'filt'}, dimensions={0}, use_global_device_ids=true | all-gather | bytes 14400 | tf_op jit(solution)/shard_map/all_gather | solution.py:188
  236.6 12.4 %copy.154 = bf16[1,640,9,640]{1,3,2,0:T(8,128)(2,1)} copy(bf16[1,640,9,640]{3,1,2,0:T(8,128)(2,1)} %all-gather.8.cloned.1.call-done) | data formatting | bytes 14745600 | tf_op jit(solution)/shard_map/all_gather | solution.py:115
  248.9 20.4 %multiply_reduce_fusion.3 = (f32[640]{0:T(1024)S(1)}, f32[1536,640]{1,0:T(8,128)}) fusion(f32[1536]{0:T(1024)S(1)} %mul.497, bf16[5760,1536]{0,1:T(8,128)(2,1)} %bitcast.334, bf16[640,5760]{0,1:T(8,128)(2,1)} %bitcast.371), kind=kOutput, calls=%fused_computation.73 | convolution fusion | flops 11326585856 | bytes 29008384 | tf_op jit(solution)/shard_map/dot_general | solution.py:116
  269.3 37.2 %psum.135 = f32[640]{0:T(1024)S(1)} all-reduce(f32[640]{0:T(1024)S(1)} %get-tuple-element.113), channel_id=1, replica_groups=mesh['batch'=4,'filt'=8] {'batch','filt'}, use_global_device_ids=true, to_apply=%region_6.7 | all-reduce | flops 640 | bytes 5120 | tf_op jit(solution)/shard_map/psum | solution.py:73
  309.1 42.1 %psum.136 = f32[640]{0:T(1024)S(1)} all-reduce(f32[640]{0:T(1024)S(1)} %multiply_reduce_fusion.2), channel_id=1, replica_groups=mesh['batch'=4,'filt'=8] {'batch','filt'}, use_global_device_ids=true, to_apply=%region_8.9 | all-reduce | flops 640 | bytes 5120 | tf_op jit(solution)/shard_map/psum | solution.py:78
  365.6 12.4 %copy.156 = bf16[1,640,9,640]{1,3,2,0:T(8,128)(2,1)} copy(bf16[1,640,9,640]{3,1,2,0:T(8,128)(2,1)} %all-gather.10.cloned.1.call-done) | data formatting | bytes 14745600 | tf_op jit(solution)/shard_map/all_gather | solution.py:115
  378.0 20.7 %multiply_reduce_fusion.1 = (f32[640]{0:T(1024)S(1)}, f32[1536,640]{1,0:T(8,128)}) fusion(f32[1536]{0:T(1024)S(1)} %mul.497, f32[1536,640]{1,0:T(8,128)} %get-tuple-element.112, bf16[5760,1536]{0,1:T(8,128)(2,1)} %bitcast.335, bf16[640,5760]{0,1:T(8,128)(2,1)} %bitcast.373), kind=kOutput, calls=%fused_computation.70 | convolution fusion | flops 11327568896 | bytes 32940544 | tf_op jit(solution)/shard_map/dot_general | solution.py:116
  398.7 38.6 %psum.137 = f32[640]{0:T(1024)S(1)} all-reduce(f32[640]{0:T(1024)S(1)} %get-tuple-element.115), channel_id=1, replica_groups=mesh['batch'=4,'filt'=8] {'batch','filt'}, use_global_device_ids=true, to_apply=%region_10.11 | all-reduce | flops 640 | bytes 5120 | tf_op jit(solution)/shard_map/psum | solution.py:73
  439.9 41.6 %psum.138 = f32[640]{0:T(1024)S(1)} all-reduce(f32[640]{0:T(1024)S(1)} %multiply_reduce_fusion), channel_id=1, replica_groups=mesh['batch'=4,'filt'=8] {'batch','filt'}, use_global_device_ids=true, to_apply=%region_12.13 | all-reduce | flops 640 | bytes 5120 | tf_op jit(solution)/shard_map/psum | solution.py:78
  493.7 38.8 %all-reduce.27 = (f32[640]{0:T(1024)S(1)}, f32[640]{0:T(1024)S(1)}) all-reduce(f32[640]{0:T(1024)S(1)} %get-tuple-element.25, f32[640]{0:T(1024)S(1)} %get-tuple-element.24), channel_id=1, replica_groups=mesh['batch'=4,'filt'=8] {'batch','filt'}, use_global_device_ids=true, to_apply=%region_23.24 | all-reduce | flops 1280 | bytes 10240 | tf_op jit(solution)/shard_map/psum | solution.py:99
  538.2 24.1 %convolution_bitcast_fusion.1 = f32[5760,1536]{0,1:T(8,128)} fusion(bf16[640,5760]{0,1:T(8,128)(2,1)} %bitcast.374, f32[640,1536]{0,1:T(8,128)} %fusion.4), kind=kOutput, calls=%fused_computation.2 | convolution fusion | flops 11325603840 | bytes 46694400 | tf_op jit(solution)/shard_map/dot_general | solution.py:137
  562.4 22.5 %fusion.63 = (f32[640,1536]{0,1:T(8,128)}, f32[640,1536]{0,1:T(8,128)S(1)}, f32[640,1536]{0,1:T(8,128)}, f32[640,1536]{0,1:T(8,128)}, f32[640,1536]{0,1:T(8,128)...) fusion(f32[5760,1536]{0,1:T(8,128)} %convolution_bitcast_fusion.1), kind=kLoop, calls=%fused_computation.220 | loop fusion | bytes 70778880 | tf_op jit(solution)/shard_map/slice | solution.py:49
  584.9 10.3 pad_add_fusion.1
  595.2 10.5 pad_add_fusion.8
  607.6 41.4 %all-reduce.26 = (f32[640]{0:T(1024)S(1)}, f32[640]{0:T(1024)S(1)}) all-reduce(f32[640]{0:T(1024)S(1)} %get-tuple-element.23, f32[640]{0:T(1024)S(1)} %get-tuple-element.22), channel_id=1, replica_groups=mesh['batch'=4,'filt'=8] {'batch','filt'}, use_global_device_ids=true, to_apply=%region_27.28 | all-reduce | flops 1280 | bytes 10240 | tf_op jit(solution)/shard_map/psum | solution.py:99
  654.6 18.0 %fusion.31 = f32[640,9,640]{2,0,1:T(8,128)} fusion(bf16[9,640,1536]{1,2,0:T(8,128)(2,1)} %constant_dynamic-update-slice_fusion.11, bf16[640,1536]{0,1:T(8,128)(2,1)S(1)} %fusion.24), kind=kOutput, calls=%fused_computation.96 | convolution fusion | flops 11324620800 | bytes 34406400 | tf_op jit(solution)/shard_map/dot_general | solution.py:126
  691.3 18.0 %fusion.29 = f32[640,9,640]{2,0,1:T(8,128)} fusion(bf16[9,640,1536]{1,2,0:T(8,128)(2,1)} %constant_dynamic-update-slice_fusion.19, f32[640,1536]{0,1:T(8,128)S(1)} %copy-done.6), kind=kOutput, calls=%fused_computation.93 | convolution fusion | flops 11325603840 | bytes 36372480 | tf_op jit(solution)/shard_map/dot_general | solution.py:126
  710.9 21.3 %convolution_bitcast_fusion = f32[5760,1536]{0,1:T(8,128)} fusion(bf16[640,1536]{0,1:T(8,128)(2,1)S(1)} %copy-done.8, bf16[640,5760]{0,1:T(8,128)(2,1)} %bitcast.372), kind=kOutput, calls=%fused_computation.1 | convolution fusion | flops 11324620800 | bytes 44728320 | tf_op jit(solution)/shard_map/dot_general | solution.py:137
  732.2 24.2 %fusion.62 = (f32[640,1536]{0,1:T(8,128)}, f32[640,1536]{0,1:T(8,128)}, f32[640,1536]{0,1:T(8,128)}, f32[640,1536]{0,1:T(8,128)}, f32[640,1536]{0,1:T(8,128)}, /...) fusion(f32[5760,1536]{0,1:T(8,128)} %convolution_bitcast_fusion), kind=kLoop, calls=%fused_computation.219 | loop fusion | bytes 70778880 | tf_op jit(solution)/shard_map/slice | solution.py:49
  774.3 41.3 %all-reduce.25 = (f32[640]{0:T(1024)S(1)}, f32[640]{0:T(1024)S(1)}) all-reduce(f32[640]{0:T(1024)S(1)} %get-tuple-element.21, f32[640]{0:T(1024)S(1)} %get-tuple-element.20), channel_id=1, replica_groups=mesh['batch'=4,'filt'=8] {'batch','filt'}, use_global_device_ids=true, to_apply=%region_31.32 | all-reduce | flops 1280 | bytes 10240 | tf_op jit(solution)/shard_map/psum | solution.py:99
  824.2 147.5 %reduce-scatter.11.cloned.1.call-done = f32[80,9,640]{2,0,1:T(8,128)} async-done(((f32[640,9,640]{2,0,1:T(8,128)}), f32[80,9,640]{2,0,1:T(8,128)}) %reduce-scatter.11.cloned.1.call-update) | async-done | bytes 1843216 | tf_op jit(solution)/shard_map/reduce_scatter | solution.py:129
  979.7 40.0 %all-reduce.24 = (f32[16,27]{1,0:T(8,128)S(1)}, f32[10]{0:T(128)S(1)}, f32[]{:T(128)}) all-reduce(f32[16,27]{1,0:T(8,128)S(1)} %fusion.36, f32[10]{0:T(128)S(1)} %copy-done.53, f32[]{:T(128)S(6)} %neg.3), channel_id=1, replica_groups=mesh['batch'=4,'filt'=8] {'batch','filt'}, use_global_device_ids=true, to_apply=%region_32.33 | all-reduce | flops 443 | bytes 3544 | tf_op jit(solution)/shard_map/psum | solution.py:278
  1021.8 11.8 reduce-scatter.13.cloned.1.call-done
  1034.4 12.9 %all-reduce.28 = (f32[80,16]{0,1:T(8,128)S(1)}, f32[10,80]{1,0:T(8,128)S(1)}) all-reduce(f32[80,16]{0,1:T(8,128)S(1)} %copy.169, f32[10,80]{1,0:T(8,128)S(1)} %copy.171), channel_id=1, replica_groups=mesh['batch'=4,'filt'=8] {'batch'}, use_global_device_ids=true, to_apply=%region_38.39 | all-reduce | flops 2080 | bytes 16640 | tf_op jit(solution)/shard_map/psum | solution.py:275
  1048.5 86.8 %all-reduce.31.cloned.1.call-done = f32[2,80,9,640]{3,1,2,0:T(8,128)} async-done(((f32[2,80,9,640]{3,1,2,0:T(8,128)}), f32[2,80,9,640]{3,1,2,0:T(8,128)}) %all-reduce.31.cloned.1.call-update) | async-done | bytes 3686416 | tf_op jit(solution)/shard_map/psum | solution.py:275
  1142.9 14.1 %psum.149 = f32[]{:T(128)} all-reduce(f32[]{:T(128)S(6)} %add.378), channel_id=1, replica_groups=mesh['batch'=4,'filt'=8] {'filt'}, use_global_device_ids=true, to_apply=%region_44.45 | all-reduce | flops 1 | bytes 8 | tf_op jit(solution)/shard_map/psum | solution.py:288
  1162.2 9.9 multiply_subtract_fusion
  (283 shorter events, 165.3 us)
Async XLA Ops:
  7.2 229.4 %all-gather.8.cloned.1.call-start = ((), (), s32[]{:S(2)}) async-start(), calls=%async_computation.7 | async-start | bytes 8294400 | tf_op jit(solution)/shard_map/all_gather | solution.py:115
  10.9 354.7 %all-gather.10.cloned.1.call-start = ((), (), s32[]{:S(2)}) async-start(), calls=%async_computation.8 | async-start | bytes 8294400 | tf_op jit(solution)/shard_map/all_gather | solution.py:115
  11.7 812.4 %reduce-scatter.9.cloned.1.call-start = ((), (), s32[]{:S(2)}) async-start(), calls=%async_computation.4 | async-start | bytes 16588800 | tf_op jit(solution)/shard_map/reduce_scatter | solution.py:129
  21.8 124.0 %copy-start.9 = (bf16[27,1536]{1,0:T(8,128)(2,1)}, bf16[27,1536]{1,0:T(8,128)(2,1)S(1)}, u32[]{:S(2)}) copy-start(bf16[27,1536]{1,0:T(8,128)(2,1)S(1)} %reshape.217) | copy-start | bytes 248836
  37.8 108.0 %copy-start.15 = (bf16[640,16]{0,1:T(8,128)(2,1)}, bf16[640,16]{0,1:T(8,128)(2,1)S(1)}, u32[]{:S(2)}) copy-start(bf16[640,16]{0,1:T(8,128)(2,1)S(1)} %reshape.252) | copy-start | bytes 61444
  52.7 93.1 %copy-start.13 = (bf16[1536,16]{0,1:T(8,128)(2,1)}, bf16[1536,16]{0,1:T(8,128)(2,1)S(1)}, u32[]{:S(2)}) copy-start(bf16[1536,16]{0,1:T(8,128)(2,1)S(1)} %convolution_convert_fusion.1) | copy-start | bytes 147460
  95.4 123.0 %copy-start.48 = (f32[768]{0:T(1024)}, f32[768]{0:T(1024)S(1)}, u32[]{:S(2)}) copy-start(f32[768]{0:T(1024)S(1)} %get-tuple-element.72) | copy-start | bytes 9220
  143.1 85.0 %copy-start.20 = (f32[640]{0:T(1024)}, f32[640]{0:T(1024)S(1)}, u32[]{:S(2)}) copy-start(f32[640]{0:T(1024)S(1)} %broadcast_divide_fusion.2) | copy-start | bytes 7684
  186.1 41.9 %copy-start.17 = (f32[640]{0:T(1024)}, f32[640]{0:T(1024)S(1)}, u32[]{:S(2)}) copy-start(f32[640]{0:T(1024)S(1)} %get-tuple-element.30) | copy-start | bytes 7684
  488.8 49.4 %copy-start.11 = (f32[640,24]{0,1:T(8,128)}, f32[640,24]{0,1:T(8,128)S(1)}, u32[]{:S(2)}) copy-start(f32[640,24]{0,1:T(8,128)S(1)} %reduce_sum.250) | copy-start | bytes 184324
  672.6 299.0 %reduce-scatter.11.cloned.1.call-start = ((), (), s32[]{:S(2)}) async-start(), calls=%async_computation.5 | async-start | bytes 16588800 | tf_op jit(solution)/shard_map/reduce_scatter | solution.py:129
  709.3 311.6 %reduce-scatter.15.cloned.1.call-start = ((), (), s32[]{:S(2)}) async-start(), calls=%async_computation.10 | async-start | bytes 368640
  772.4 43.2 %copy-start.12 = (f32[640,24]{0,1:T(8,128)S(1)}, f32[640,24]{0,1:T(8,128)}, u32[]{:S(2)}) copy-start(f32[640,24]{0,1:T(8,128)} %copy-done.11) | copy-start | bytes 184324
  772.4 43.2 %copy-start.27 = (bf16[10,24]{1,0:T(8,128)(2,1)S(1)}, bf16[10,24]{1,0:T(8,128)(2,1)}, u32[]{:S(2)}) copy-start(bf16[10,24]{1,0:T(8,128)(2,1)} %copy-done.26) | copy-start | bytes 1444
  772.4 44.3 %copy-start.34 = (f32[640]{0:T(1024)S(1)}, f32[640]{0:T(1024)}, u32[]{:S(2)}) copy-start(f32[640]{0:T(1024)} %get-tuple-element.65) | copy-start | bytes 7684
  816.6 216.9 %reduce-scatter.13.cloned.1.call-start = ((), (), s32[]{:S(2)}) async-start(), calls=%async_computation.9 | async-start | bytes 368640
  823.9 311.5 %all-reduce.31.cloned.1.call-start = ((), (), s32[]{:S(2)}) async-start(), calls=%async_computation.6 | async-start | bytes 7372800 | tf_op jit(solution)/shard_map/psum | solution.py:275
  975.9 183.2 %copy-start.52 = (f32[10]{0:T(128)S(1)}, f32[10]{0:T(128)}, u32[]{:S(2)}) copy-start(f32[10]{0:T(128)} %param.33) | copy-start | bytes 124
  975.9 183.1 %copy-start.56 = (f32[10]{0:T(128)S(1)}, f32[10]{0:T(128)}, u32[]{:S(2)}) copy-start(f32[10]{0:T(128)} %param.44) | copy-start | bytes 124
  975.9 183.1 %copy-start.57 = (f32[10]{0:T(128)S(1)}, f32[10]{0:T(128)}, u32[]{:S(2)}) copy-start(f32[10]{0:T(128)} %param.45) | copy-start | bytes 124
  975.9 183.7 %copy-start.31 = (f32[10,80]{1,0:T(8,128)S(1)}, f32[10,80]{1,0:T(8,128)}, u32[]{:S(2)}) copy-start(f32[10,80]{1,0:T(8,128)} %param.32) | copy-start | bytes 9604
  975.9 183.7 %copy-start.41 = (f32[10,80]{1,0:T(8,128)S(1)}, f32[10,80]{1,0:T(8,128)}, u32[]{:S(2)}) copy-start(f32[10,80]{1,0:T(8,128)} %param.42) | copy-start | bytes 9604
  976.0 183.7 %copy-start.42 = (f32[10,80]{1,0:T(8,128)S(1)}, f32[10,80]{1,0:T(8,128)}, u32[]{:S(2)}) copy-start(f32[10,80]{1,0:T(8,128)} %param.43) | copy-start | bytes 9604
  976.0 184.3 %copy-start.40 = (f32[6,80]{1,0:T(8,128)S(1)}, f32[6,80]{1,0:T(8,128)}, u32[]{:S(2)}) copy-start(f32[6,80]{1,0:T(8,128)} %param.31) | copy-start | bytes 5764
  976.0 184.3 %copy-start.49 = (f32[6,80]{1,0:T(8,128)S(1)}, f32[6,80]{1,0:T(8,128)}, u32[]{:S(2)}) copy-start(f32[6,80]{1,0:T(8,128)} %param.40) | copy-start | bytes 5764
  976.0 184.3 %copy-start.50 = (f32[6,80]{1,0:T(8,128)S(1)}, f32[6,80]{1,0:T(8,128)}, u32[]{:S(2)}) copy-start(f32[6,80]{1,0:T(8,128)} %param.41) | copy-start | bytes 5764
  976.0 185.0 %copy-start.33 = (f32[80,16]{0,1:T(8,128)S(1)}, f32[80,16]{0,1:T(8,128)}, u32[]{:S(2)}) copy-start(f32[80,16]{0,1:T(8,128)} %param.29) | copy-start | bytes 15364
  976.0 184.9 %copy-start.43 = (f32[80,16]{0,1:T(8,128)S(1)}, f32[80,16]{0,1:T(8,128)}, u32[]{:S(2)}) copy-start(f32[80,16]{0,1:T(8,128)} %param.36) | copy-start | bytes 15364
  976.0 184.9 %copy-start.44 = (f32[80,16]{0,1:T(8,128)S(1)}, f32[80,16]{0,1:T(8,128)}, u32[]{:S(2)}) copy-start(f32[80,16]{0,1:T(8,128)} %param.37) | copy-start | bytes 15364
  976.0 185.6 %copy-start.29 = (f32[16,27]{1,0:T(8,128)S(1)}, f32[16,27]{1,0:T(8,128)}, u32[]{:S(2)}) copy-start(f32[16,27]{1,0:T(8,128)} %param.28) | copy-start | bytes 5188
  976.0 185.6 %copy-start.45 = (f32[16,27]{1,0:T(8,128)S(1)}, f32[16,27]{1,0:T(8,128)}, u32[]{:S(2)}) copy-start(f32[16,27]{1,0:T(8,128)} %param.34) | copy-start | bytes 5188
  976.1 185.5 %copy-start.46 = (f32[16,27]{1,0:T(8,128)S(1)}, f32[16,27]{1,0:T(8,128)}, u32[]{:S(2)}) copy-start(f32[16,27]{1,0:T(8,128)} %param.35) | copy-start | bytes 5188
  (35 other events, 397.0 us)
Sparse Core Ops, SparseCore 0:
  11.0 77.4 all-gather.7
  90.7 73.2 all-gather.9
  672.8 148.6 reduce-scatter.8
  823.6 148.0 reduce-scatter.10
  974.3 27.6 reduce-scatter.14
  1004.8 28.6 reduce-scatter.12
  1037.3 98.0 all-reduce.30
where the time goes:
time: 1190 us; the launch traced here: 1180 us
  blocking collectives  520 us (44%)
  waiting for transfers between devices  247 us (21%)
  local copies, waits for them, and re-layouts  146 us (12%)
  matrix products  129 us (11%)
  other arithmetic  113 us (9%)
  between operations  25.1 us (2%)
    reduce_scatter x2, waiting for transfers between devices, conv_backward(): lax.psum_scatter(term.reshape(lax.axis_size('filt') * weight_shard.shape[...  148 us
    psum x3, blocking collectives, norm_forward(): lax.psum(jnp.sum(centered_input * centered_input * row_validity_mask, axi...  124 us
    psum x3, blocking collectives, masked_norm_backward(): lax.psum((jnp.sum(passed_rows, axis=1), jnp.sum(passed_rows * normalized_...  121 us
    psum x3, blocking collectives, norm_forward(): lax.psum(jnp.sum(feature_field * row_validity_mask, axis=1), ('batch', 'f...  120 us
    psum x1, waiting for transfers between devices, body(): lax.psum((jnp.stack([conv_grad_zero, conv_grad_one]), bridge_part, head_p...  86.8 us
    unnamed x168, local copies, waits for them, and re-layouts  52.5 us
    slice x2, local copies, waits for them, and re-layouts, unshifted(): grid[3 * row_off + col_off]  46.8 us
    dot_general x2, matrix products, conv_backward(): lax.dot_general(piece.reshape(piece.shape[0], -1), rows_grad, (((0,), (0,...  45.5 us
  transfers between devices with their start and end apart: 7, of which 3 were waited for; matrix products, arithmetic and copies ran while one was open for 18% of the time, Pallas kernels for 0%

commit v1 on v0

--- a/solution.py
+++ b/solution.py
@@ -1,10 +1,11 @@
 import jax
 import jax.numpy as jnp
 from jax import lax
+from jax.experimental import pallas as pl
+from jax.experimental.pallas import tpu as pltpu
 from jax.sharding import PartitionSpec as P
 
 STEP = 8
-
 
 beta_one = 0.9
 beta_two = 0.95
@@ -12,6 +13,929 @@
 norm_epsilon = 1e-05
 clip_norm = 0.01
 own_share = 0.7
+
+MESH = pl.DeviceIdType.MESH
+bf16 = jnp.bfloat16
+f32 = jnp.float32
+LINE = bf16
+NB, NF, NZ, NDEV, NCHIP = 4, 8, 4, 32, 16
+C, IMG, ROWS = 640, 24, 1536
+BLK = 8 * IMG
+AC = (((1,), (1,)), ((), ()))
+CC = (((0,), (0,)), ((), ()))
+
+
+def iota(shape, dim):
+    return lax.broadcasted_iota(jnp.int32, shape, dim)
+
+
+def wide(row5):
+    return jnp.concatenate([row5[k : k + 1, :] for k in range(5)], axis=1)
+
+
+def column(row, n):
+    eye = iota((n, n), 0) == iota((n, n), 1)
+    return jnp.sum(jnp.where(eye, jnp.broadcast_to(row, (n, n)), 0.0), axis=1, keepdims=True)
+
+
+class Place:
+    def __init__(self):
+        self.b = lax.axis_index("batch")
+        self.f = lax.axis_index("filt")
+        self.z = self.f // 2
+        self.c = lax.rem(self.f, 2)
+        self.me = self.b * NF + self.f
+        self.chip = self.b * NZ + self.z
+        self.xn = self.b + 1 - 2 * lax.rem(self.b, 2)
+        self.yn = lax.rem(self.b + 2, NB)
+        self.dn = (NB - 1) - self.b
+        self.sib = self.f + 1 - 2 * self.c
+
+
+def remote(src, dst, ssem, rsem, b, f):
+    return pltpu.make_async_remote_copy(
+        src_ref=src, dst_ref=dst, send_sem=ssem, recv_sem=rsem, device_id=(b, f), device_id_type=MESH
+    )
+
+
+def greet(p):
+    sem = pltpu.get_barrier_semaphore()
+
+    def hello(i, carry):
+        to = lax.rem(p.me + i, NDEV)
+        pl.semaphore_signal(
+            sem, inc=1, device_id=(to // NF, lax.rem(to, NF)), device_id_type=MESH
+        )
+        return carry
+
+    lax.fori_loop(1, NDEV, hello, 0)
+
+
+def met():
+    pl.semaphore_wait(pltpu.get_barrier_semaphore(), NDEV - 1)
+
+
+class Exchange:
+    def __init__(self, p, slots, sibs, ssem, rsem, psem, qsem):
+        self.p, self.slots, self.sibs = p, slots, sibs
+        self.ssem, self.rsem, self.psem, self.qsem = ssem, rsem, psem, qsem
+
+    def mine(self, e):
+        return self.slots.at[e, self.p.chip]
+
+    def send(self, e):
+        p = self.p
+        mine = self.mine(e)
+
+        def one(i, carry):
+            to = lax.rem(p.chip + i, NCHIP)
+            remote(
+                mine, mine, self.ssem.at[e], self.rsem.at[e], to // NZ, 2 * lax.rem(to, NZ) + p.c
+            ).start()
+            return carry
+
+        lax.fori_loop(1, NCHIP, one, 0)
+
+    def wait(self, e):
+        p = self.p
+        rest = self.slots.at[e, 0 : NCHIP - 1]
+        remote(rest, rest, self.ssem.at[e], self.rsem.at[e], p.b, p.sib).wait()
+
+    def swap(self, e, value):
+        p = self.p
+        self.sibs[e, 0] = value
+        copy = remote(
+            self.sibs.at[e, 0], self.sibs.at[e, 1], self.psem.at[e], self.qsem.at[e], p.b, p.sib
+        )
+        copy.start()
+        copy.wait()
+        return self.sibs[e, 1]
+
+    def total(self, e):
+        self.wait(e)
+        own = jnp.sum(self.slots[e], axis=0)
+        return own + self.swap(e, own)
+
+
+def put_row(slot, row, value):
+    for k in range(5):
+        slot[row + k : row + k + 1, :] = value[:, 128 * k : 128 * k + 128]
+
+
+def put_spare(slot, value):
+    for k, row in enumerate((5, 6, 7, 13, 14)):
+        slot[row : row + 1, :] = value[:, 128 * k : 128 * k + 128]
+
+
+def spare(rows):
+    return wide(jnp.concatenate([rows[5:8], rows[13:15]], axis=0))
+
+
+def local_stats(src, mask, count, slot):
+    def total(j, acc):
+        x = src[pl.ds(pl.multiple_of(j * BLK, BLK), BLK), :]
+        m = jnp.concatenate([mask[...]] * 5, axis=1)
+        return acc + jnp.sum((x * m).reshape(BLK // 8, 8, C), axis=0)
+
+    acc = lax.fori_loop(0, 8, total, jnp.zeros((8, C), f32))
+    own_sum = jnp.sum(acc, axis=0, keepdims=True)
+    own_mean = own_sum / jnp.maximum(count, 1.0)
+
+    def squares(j, acc):
+        x = src[pl.ds(pl.multiple_of(j * BLK, BLK), BLK), :]
+        m = jnp.concatenate([mask[...]] * 5, axis=1)
+        d = x - own_mean
+        return acc + jnp.sum((d * d * m).reshape(BLK // 8, 8, C), axis=0)
+
+    acc = lax.fori_loop(0, 8, squares, jnp.zeros((8, C), f32))
+    put_row(slot, 0, own_sum)
+    put_row(slot, 8, jnp.sum(acc, axis=0, keepdims=True))
+
+
+def joint_stats(ex, e):
+    ex.wait(e)
+    every = ex.slots[e]
+    n = ex.slots[0, :, 5:6, :]
+    sums = every[:, 0:5, :]
+    n_own, s_own = jnp.sum(n, axis=0), jnp.sum(sums, axis=0)
+    m_own = s_own / jnp.maximum(n_own, 1.0)
+    off = sums / jnp.maximum(n, 1.0) - m_own[None]
+    q_own = jnp.sum(every[:, 8:13, :] + n * off * off, axis=0)
+    rest = jnp.sum(every[:, 5:8, :], axis=0)
+    more = jnp.sum(every[:, 13:16, :], axis=0)
+    got = ex.swap(e, jnp.concatenate([s_own, rest, q_own, more], axis=0))
+    n_sib = ex.sibs[0, 1, 5:6, :]
+    s_sib, q_sib = got[0:5], got[8:13]
+    count = n_own + n_sib
+    mean = (s_own + s_sib) / count
+    a, b = m_own - mean, s_sib / jnp.maximum(n_sib, 1.0) - mean
+    spread = ((q_own + q_sib) + (n_own * a * a + n_sib * b * b)) / count
+    return wide(mean), wide(lax.rsqrt(spread + norm_epsilon)), spare(got + jnp.concatenate([s_own, rest, q_own, more], axis=0))
+
+
+def spread_rows(S, j, x):
+    at = pl.ds(pl.multiple_of((j + 1) * BLK, BLK), BLK)
+    gap = jnp.zeros((IMG, C), f32)
+    S[0, at, :] = jnp.concatenate([gap, x[: BLK - IMG]], axis=0).astype(bf16)
+    S[1, at, :] = x.astype(bf16)
+    S[2, at, :] = jnp.concatenate([x[IMG:], gap], axis=0).astype(bf16)
+
+
+def conv_rows(S, W, k, r0, M):
+    acc = None
+    for u in range(3):
+        lhs = jnp.concatenate([S[u, pl.ds(r0 + v * BLK, M), :] for v in range(3)], axis=1)
+        rhs = jnp.concatenate(
+            [
+                jnp.concatenate(
+                    [W[k, u, z, c, v * 80 : v * 80 + 80, :] for z in range(NZ) for c in range(2)], axis=0
+                )
+                for v in range(3)
+            ],
+            axis=1,
+        )
+        d = lax.dot_general(lhs, rhs, AC, preferred_element_type=f32)
+        acc = d if acc is None else acc + d
+    return acc
+
+
+class Gather:
+    def __init__(self, p, W, zs, zr, xs, xr, ds, dr):
+        self.p, self.W = p, W
+        self.zs, self.zr, self.xs, self.xr, self.ds, self.dr = zs, zr, xs, xr, ds, dr
+
+    def part(self, s, z, b, row, n):
+        return self.W.at[
+            s // 3, lax.rem(s, 3), z, self.p.c, pl.ds(pl.multiple_of(b * 64 + row, 32), n), :
+        ]
+
+    def zcopy(self, s, i):
+        p = self.p
+        mine = self.part(s, p.z, p.b, 0, 64)
+        to = lax.rem(p.z + i, NZ)
+        return remote(mine, mine, self.zs.at[s, i], self.zr.at[s, i], p.b, 2 * to + p.c)
+
+    def zsend(self, s):
+        for i in (2, 1, 3):
+            self.zcopy(s, i).start()
+
+    def xcopy(self, s, i, d):
+        p = self.p
+        z = lax.rem(p.z + NZ - i, NZ)
+        b, row, n, to = ((p.b, 0, 64, p.xn), (p.b, 0, 64, p.yn), (p.xn, 0, 32, p.yn), (p.yn, 32, 32, p.xn))[d]
+        part = self.part(s, z, b, row, n)
+        at = 3 * d + i - 1
+        return remote(part, part, self.xs.at[s, at], self.xr.at[s, at], to, p.f)
+
+    def relay(self, s):
+        for i in range(1, NZ):
+            self.zcopy(s, i).wait_recv()
+            self.xcopy(s, i, 0).start()
+            self.xcopy(s, i, 1).start()
+
+    def turn(self, s):
+        for i in range(1, NZ):
+            self.xcopy(s, i, 0).wait_recv()
+            self.xcopy(s, i, 2).start()
+            self.xcopy(s, i, 1).wait_recv()
+            self.xcopy(s, i, 3).start()
+
+    def dcopy(self, s):
+        p = self.p
+        mine = self.W.at[s // 3, lax.rem(s, 3), :, p.c]
+        return remote(mine, mine, self.ds.at[s], self.dr.at[s], p.b, p.sib)
+
+    def across(self, s):
+        for i in range(1, NZ):
+            self.xcopy(s, i, 2).wait_recv()
+            self.xcopy(s, i, 3).wait_recv()
+        self.dcopy(s).start()
+
+    def arrive(self, s):
+        self.dcopy(s).wait_recv()
+
+    def drain(self, s):
+        for i in range(1, NZ):
+            self.zcopy(s, i).wait_send()
+            for d in range(4):
+                self.xcopy(s, i, d).wait_send()
+        self.dcopy(s).wait_send()
+
+
+class Scatter:
+    def __init__(self, p, W, RX, RZ, G, Q, GF, sems):
+        self.p, self.W, self.RX, self.RZ, self.G, self.Q, self.GF = p, W, RX, RZ, G, Q, GF
+        (self.bs, self.br, self.cs, self.cr, self.es, self.er) = sems
+
+    def held(self, e, q, half):
+        return self.G.at[e % 3, :, pl.ds(pl.multiple_of(q * 64 + 32 * half, 32), 32), :]
+
+    def room(self, e, i):
+        at = pl.ds(128 * (i % 2), 128)
+        if e < 3:
+            ref = self.RX.at[e, i // 2, at, :]
+        else:
+            ref = self.W.at[1, e % 3, i // 4, (i // 2) % 2, at, :]
+        return ref
+
+    def hop(self, e, i):
+        p = self.p
+        q, half, to = (
+            (p.dn, 0, p.xn), (p.dn, 1, p.yn), (p.xn, 0, p.xn), (p.yn, 1, p.yn), (p.yn, 0, p.yn), (p.xn, 1, p.xn),
+        )[i]
+        return remote(
+            self.held(e, q, half), self.room(e, i).reshape(NZ, 32, C), self.bs.at[e, i], self.br.at[e, i], to, p.f
+        )
+
+    def begin(self, e):
+        for i in range(4):
+            self.hop(e, i).start()
+
+    def mid(self, e):
+        p = self.p
+        for i, q, half in ((0, p.yn, 0), (1, p.xn, 1)):
+            self.hop(e, i).wait_recv()
+            mine = self.held(e, q, half)
+            got = self.room(e, i)[...].reshape(NZ, 32, C).astype(f32)
+            mine[...] = (mine[...].astype(f32) + got).astype(bf16)
+            self.hop(e, 4 + i).start()
+
+    def out3(self, e, i):
+        p = self.p
+        to = lax.rem(p.z + i, NZ)
+        return remote(
+            self.Q.at[e % 3, to], self.RZ.at[e, i - 1], self.cs.at[e, i - 1], self.cr.at[e, i - 1], p.b, 2 * to + p.c
+        )
+
+    def out4(self, e, d):
+        p = self.p
+        to = (p.xn, p.yn, p.dn)[d]
+        mine = self.GF.at[1 - e // 3, e % 3, pl.ds(pl.multiple_of(p.b * 64, 64), 64), :]
+        return remote(mine, mine, self.es.at[e, d], self.er.at[e, d], to, p.f)
+
+    def along(self, e):
+        p = self.p
+        for i in range(2, 6):
+            self.hop(e, i).wait_recv()
+        for half, ways in ((0, (2, 4)), (1, (3, 5))):
+            acc = self.held(e, p.b, half)[...].astype(f32)
+            for i in ways:
+                acc = acc + self.room(e, i)[...].reshape(NZ, 32, C).astype(f32)
+            self.Q[e % 3, :, 32 * half : 32 * half + 32, :] = acc.astype(self.Q.dtype)
+        for i in (2, 1, 3):
+            self.out3(e, i).start()
+
+    def final(self, e, lost):
+        p = self.p
+        for i in range(1, NZ):
+            self.out3(e, i).wait_recv()
+        acc = self.Q[e % 3, p.z].astype(f32)
+        for i in range(1, NZ):
+            acc = acc + self.RZ[e, i - 1].astype(f32)
+        acc = acc + lost
+        low = acc.astype(bf16)
+        self.GF[1 - e // 3, e % 3, pl.ds(pl.multiple_of(p.b * 64, 64), 64), :] = low
+        for d in (2, 0, 1):
+            self.out4(e, d).start()
+        low = low.astype(f32)
+        return jnp.sum((low * low).reshape(8, 8, C), axis=0)
+
+    def clear(self, e):
+        for i in range(6):
+            self.hop(e, i).wait_send()
+        for i in range(1, NZ):
+            self.out3(e, i).wait_send()
+
+    def end(self, e):
+        for d in range(3):
+            self.out4(e, d).wait()
+
+
+def conv_back_rows(S, W, k, r0, M):
+    acc = None
+    for u in range(3):
+        lhs = jnp.concatenate([S[2 - u, pl.ds(r0 + (2 - v) * BLK, M), :] for v in range(3)], axis=1)
+        rhs = jnp.concatenate(
+            [
+                W[k, u, z, c, v * 80 : v * 80 + 80, :]
+                for v in range(3)
+                for z in range(NZ)
+                for c in range(2)
+            ],
+            axis=0,
+        )
+        d = jnp.dot(lhs, rhs, preferred_element_type=f32)
+        acc = d if acc is None else acc + d
+    return acc
+
+
+def filter_grad(p, S, S2, dyT, dyS, DS, mu, G, e):
+    u = e % 3
+    if u == 0:
+        ones = jnp.ones((ROWS, 128), bf16)
+        own = jnp.concatenate([dyT[z, p.c] for z in range(NZ)], axis=0)
+        sib = jnp.concatenate([dyS[z] for z in range(NZ)], axis=0)
+        DS[...] = jnp.dot(own, ones, preferred_element_type=f32) + jnp.dot(
+            sib, ones, preferred_element_type=f32
+        )
+
+    def tap(v, carry):
+        at = pl.ds(pl.multiple_of(v * BLK, BLK), ROWS)
+        own = jnp.concatenate([dyT[z, p.c] for z in range(NZ)], axis=0)
+        sib = jnp.concatenate([dyS[z] for z in range(NZ)], axis=0)
+        d = jnp.dot(own, S[u, at, :], preferred_element_type=f32)
+        d = d + jnp.dot(sib, S2[u, at, :], preferred_element_type=f32)
+        d = d - jnp.concatenate([DS[...]] * 5, axis=1) * mu
+        for z in range(NZ):
+            G[u, z, pl.ds(pl.multiple_of(v * 80, 16), 80), :] = d[80 * z : 80 * z + 80].astype(bf16)
+        return carry
+
+    lax.fori_loop(0, 3, tap, 0)
+
+
+def step_kernel(
+    images, labels, partner, valid, sizes, stem_w, bridge_t, conv_w, norm, head, bias,
+    GF, bh_o, small_o, norm_o, misc_o,
+    W, S, S2, dyT, dyS, DS, inner, block, dfl, RX, RZ, G, Q, slots, sibs, lab, gath, par, mask, AB, stem, dstem, pad,
+    xs_, xr_, ps_, pr_, lbs, lbr, gs, gr, zs, zr, xs, xr, ds, dr, ls,
+    bs, br, cs, cr, es, er, ts, tr, us, ur, free, fs, fr, hs, hr, js, jr, ms, mr,
+):
+    p = Place()
+    ex = Exchange(p, slots, sibs, xs_, xr_, ps_, pr_)
+    ga = Gather(p, W, zs, zr, xs, xr, ds, dr)
+    sc = Scatter(p, W, RX, RZ, G, Q, GF, (bs, br, cs, cr, es, er))
+    greet(p)
+    load = pltpu.make_async_copy(conv_w.reshape(1440, C), block.at[pl.ds(0, 1440)], ls.at[0])
+    load.start()
+    mine = gath.at[p.f]
+    mine[...] = jnp.zeros((40, 128), f32)
+    mine[0:16, 0:80] = bridge_t[...]
+    mine[16:22, 0:80] = norm[...]
+    mine[24:34, 0:80] = head[...]
+    def small(i):
+        to = lax.rem(p.f + i, NF)
+        return remote(mine, mine, gs, gr, p.b, to)
+
+    def cast(s):
+        k, u = s // 3, s % 3
+        for v in range(3):
+            t = 9 * k + 3 * u + v
+            W[k, u, p.z, p.c, 80 * v : 80 * v + 80, :] = block[80 * t : 80 * t + 80, :].astype(bf16)
+        W[k, u, p.z, p.c, 240:256, :] = jnp.zeros((16, C), bf16)
+
+    load.wait()
+    cast(0)
+    met()
+    for i in range(1, NF):
+        small(i).start()
+    ga.zsend(0)
+    for s in range(1, 6):
+        cast(s)
+        if s < 3:
+            ga.zsend(s)
+    img = pltpu.roll(images[...].astype(f32), 32, 1)
+    lane = iota((IMG, 128), 1)
+    for c in range(3):
+        for i in range(8):
+            a = img[:, 1024 * c + 128 * i : 1024 * c + 128 * i + 128]
+            if i == 0:
+                a = jnp.where(lane < 32, 0.0, a)
+            AB[IMG * i : IMG * i + IMG, 128 * c : 128 * c + 128] = a
+    tile_c = jnp.bitwise_and(iota((16, 128), 1), 15) == iota((16, 128), 0)
+    wc = lax.dot_general(
+        stem_w[...].astype(bf16), tile_c.astype(bf16), CC, preferred_element_type=f32
+    )
+    fold_r = (jnp.bitwise_and(iota((256, 27), 0), 31) == iota((256, 27), 1)).astype(bf16)
+    own_j = iota((256, 128), 0) // 32 == iota((256, 128), 1) // 16
+    bd = jnp.dot(fold_r, wc.astype(bf16), preferred_element_type=f32)
+    bd = jnp.where(own_j, bd, 0.0).astype(bf16)
+    l, r = iota((128, 256), 0), iota((128, 256), 1)
+    v = jnp.bitwise_and(l, 31) - 4 * (r // 32) + 1
+
+    def hits(c):
+        want = 9 * c + 3 * (l // 32) + v
+        hit = (l < 96) & (v >= 0) & (v < 3) & (want == jnp.bitwise_and(r, 31))
+        return hit.astype(f32)
+
+    acc = None
+    for c in range(3):
+        t = jnp.dot(hits(c).astype(bf16), bd, preferred_element_type=f32).astype(bf16)
+        d = jnp.dot(
+            AB[:, 128 * c : 128 * c + 128].astype(bf16), t, preferred_element_type=f32
+        )
+        acc = d if acc is None else acc + d
+    stem[...] = acc.astype(bf16).astype(f32)
+    ok = column(valid[...].astype(f32), IMG)
+    q = p.f * IMG + iota((IMG, 1), 0)
+    member = jnp.zeros((IMG, 1), jnp.int32)
+    end = jnp.int32(0)
+    for g in range(8):
+        end = end + sizes[p.b, g]
+        member = member + (q >= end).astype(jnp.int32)
+    member = jnp.minimum(member, 7)
+    size = jnp.zeros((IMG, 1), f32)
+    for g in range(8):
+        size = size + jnp.where(member == g, sizes[p.b, g].astype(f32), 0.0)
+    weight = ok / size
+    mask[...] = jnp.concatenate([jnp.broadcast_to(ok, (IMG, 128))] * 8, axis=0)
+    count = 64.0 * jnp.sum(ok)
+    own_row = labels[...].astype(f32)
+    slot = ex.mine(0)
+    slot[5:6, :] = jnp.full((1, 128), count, f32)
+    slot[6:7, :] = jnp.concatenate([own_row, jnp.zeros((1, 104), f32)], axis=1)
+    slot[7:8, :] = jnp.full((1, 128), jnp.sum(weight), f32)
+    edge = jnp.zeros((BLK, C), bf16)
+    for u in range(3):
+        S[u, 0:BLK, :] = edge
+        S[u, 9 * BLK : 10 * BLK, :] = edge
+        for z in range(NZ):
+            G[u, z, 240:256, :] = jnp.zeros((16, C), bf16)
+    rest = gath.at[0 : NF - 1]
+    remote(rest, rest, gs, gr, p.b, p.sib).wait()
+    lane = iota((40, 128), 1)
+    for k in range(5):
+        acc = jnp.zeros((40, 128), f32)
+        for f in range(NF):
+            lo, hi = max(80 * f, 128 * k), min(80 * f + 80, 128 * k + 128)
+            if lo < hi:
+                turned = pltpu.roll(gath[f], (80 * f - 128 * k) % 128, 1)
+                acc = jnp.where((lane >= lo - 128 * k) & (lane < hi - 128 * k), turned, acc)
+        par[:, 128 * k : 128 * k + 128] = acc
+    bridge8 = jnp.concatenate([par[0:16, :].astype(bf16)] * 8, axis=0)
+
+    def rows(j):
+        return pl.ds(pl.multiple_of(j * BLK, BLK), BLK)
+
+    def base_rows(j):
+        pick = iota((BLK, 128), 1) // 16 == j
+        x = jnp.where(pick, stem[...], 0.0).astype(bf16)
+        return jnp.dot(x, bridge8, preferred_element_type=f32)
+
+    def base_block(j, carry):
+        inner[rows(j), :] = base_rows(j)
+        return carry
+
+    lax.fori_loop(0, 8, base_block, 0)
+    local_stats(inner, mask, count, ex.mine(0))
+    ex.send(0)
+    ga.relay(0)
+    ga.relay(1)
+    ga.turn(0)
+
+    def inner_rows(j):
+        return inner[rows(j), :]
+
+    def block_rows(j):
+        return block[rows(j), :]
+
+    def dfl_rows(j):
+        return dfl[rows(j), :]
+
+    def gain(k):
+        return par[16 + 2 * k : 17 + 2 * k, :]
+
+    def shift(k):
+        return par[17 + 2 * k : 18 + 2 * k, :]
+
+    def normed(src, stats, k):
+        mean, scale = stats[:2]
+
+        def one(j, acc):
+            hat = (src(j) - mean) * scale
+            out = jnp.maximum(gain(k) * hat + shift(k), 0.0)
+            spread_rows(S, j, out)
+            m = jnp.concatenate([mask[...]] * 5, axis=1)
+            return acc + jnp.sum((out * m).reshape(BLK // 8, 8, C), axis=0)
+
+        acc = lax.fori_loop(0, 8, one, jnp.zeros((8, C), f32))
+        return jnp.sum(acc, axis=0, keepdims=True)
+
+    stats0 = joint_stats(ex, 0)
+    labs = remote(lab.at[0], lab.at[1], lbs, lbr, p.b, p.sib)
+    lab[0] = slots[0, :, 6, :]
+    labs.start()
+    put_spare(ex.mine(1), normed(inner_rows, stats0, 0))
+    for s in range(3, 6):
+        ga.zsend(s)
+    ga.relay(2)
+    ga.turn(1)
+    ga.across(0)
+    ga.turn(2)
+    ga.relay(3)
+    ga.across(1)
+    ga.across(2)
+    ga.relay(4)
+    for s in range(3):
+        ga.arrive(s)
+
+    def conv0(it, carry):
+        r0 = pl.multiple_of(it * 384, 384)
+        inner[pl.ds(r0, 384), :] = conv_rows(S, W, 0, r0, 384)
+
+        @pl.when(it == 0)
+        def _():
+            ga.relay(5)
+
+        @pl.when(it == 1)
+        def _():
+            ga.turn(3)
+            ga.turn(4)
+
+        @pl.when(it == 3)
+        def _():
+            ga.turn(5)
+            ga.across(3)
+
+        return carry
+
+    lax.fori_loop(0, 4, conv0, 0)
+    local_stats(inner, mask, count, ex.mine(1))
+    ex.send(1)
+    ga.across(4)
+    stats1 = joint_stats(ex, 1)
+    put_spare(ex.mine(2), normed(inner_rows, stats1, 1))
+    ga.across(5)
+    for s in range(3, 6):
+        ga.arrive(s)
+
+    def share(u):
+        return remote(S.at[u], S2.at[u], ts.at[u], tr.at[u], p.b, p.sib)
+
+    for u in range(3):
+        share(u).start()
+
+    def conv1(it, carry):
+        r0 = pl.multiple_of(it * 384, 384)
+        at = pl.ds(r0, 384)
+        low = jnp.concatenate([base_rows(2 * it), base_rows(2 * it + 1)], axis=0)
+        block[at, :] = low + conv_rows(S, W, 1, r0, 384)
+        return carry
+
+    lax.fori_loop(0, 4, conv1, 0)
+    local_stats(block, mask, count, ex.mine(2))
+    ex.send(2)
+    for s in range(6):
+        ga.drain(s)
+    lane = iota((IMG, 16), 1)
+    label = column(own_row, IMG)
+    mate = column(partner[...].astype(f32), IMG)
+    home = jnp.floor((mate + 0.5) / 24.0)
+    chip = jnp.floor((home + 0.5) / 2.0)
+    at_chip = (iota((IMG, NCHIP), 1).astype(f32) == chip).astype(bf16)
+    labs.wait()
+    own_side = jnp.dot(at_chip, lab[0].astype(bf16), preferred_element_type=f32)
+    sib_side = jnp.dot(at_chip, lab[1].astype(bf16), preferred_element_type=f32)
+    there = jnp.where(home - 2.0 * chip == p.c.astype(f32), own_side, sib_side)
+    spot = iota((IMG, 128), 1).astype(f32) == mate - 24.0 * home
+    mate_label = jnp.sum(jnp.where(spot, there, 0.0), axis=1, keepdims=True)
+    lane_f = lane.astype(f32)
+    target = own_share * (lane_f == label).astype(f32) + (1.0 - own_share) * (
+        lane_f == mate_label
+    ).astype(f32)
+    live = lane < 10
+    head16 = par[24:40, :].astype(bf16)
+    pad[...] = jnp.zeros((8, 128), f32)
+    pad[0:1, 0:10] = bias[...]
+    sides = sibs[0, 0] + sibs[0, 1]
+    total = jnp.sum(sides[7:8, 0:1])
+    valid_count = jnp.sum(sides[5:6, 0:1])
+    stats2 = joint_stats(ex, 2)
+    mu0, mu1 = stats1[2] / valid_count, stats2[2] / valid_count
+
+    def pool(j, acc):
+        hat = (block_rows(j) - stats2[0]) * stats2[1]
+        out = jnp.maximum(gain(2) * hat + shift(2), 0.0)
+        return acc + jnp.sum(out.reshape(8, IMG, C), axis=0)
+
+    pooled = lax.fori_loop(0, 8, pool, jnp.zeros((IMG, C), f32)) / 64.0
+    pooled = pooled.astype(bf16)
+    logits = lax.dot_general(pooled, head16, AC, preferred_element_type=f32) + pad[0:1, 0:16]
+    top = jnp.max(jnp.where(live, logits, -3e38), axis=1, keepdims=True)
+    moved = jnp.where(live, logits - top, 0.0)
+    size_sum = jnp.sum(jnp.where(live, jnp.exp(moved), 0.0), axis=1, keepdims=True)
+    logp = moved - jnp.log(size_sum)
+    loss_part = -jnp.sum(
+        weight * jnp.sum(jnp.where(live, target * logp, 0.0), axis=1, keepdims=True)
+    )
+    d_logits = jnp.where(live, (jnp.exp(logp) - target) * (weight / total), 0.0).astype(bf16)
+    g_bias = jnp.sum(d_logits.astype(f32), axis=0, keepdims=True)
+    par[24:40, :] = lax.dot_general(d_logits, pooled, CC, preferred_element_type=f32)
+    d_pooled = jnp.dot(d_logits, head16, preferred_element_type=f32)
+    d_out24 = d_pooled / 64.0
+
+    def zhat(src, j, stats):
+        return (src(j) - stats[0]) * stats[1]
+
+    def passed(hat, k, d_out):
+        return jnp.where(gain(k) * hat + shift(k) > 0.0, d_out, 0.0)
+
+    def grad_sums(src, stats, k, d_of, e):
+        def one(j, acc):
+            hat = zhat(src, j, stats)
+            got = passed(hat, k, d_of(j))
+            return (
+                acc[0] + jnp.sum(got.reshape(BLK // 8, 8, C), axis=0),
+                acc[1] + jnp.sum((got * hat).reshape(BLK // 8, 8, C), axis=0),
+            )
+
+        zero = jnp.zeros((8, C), f32)
+        acc = lax.fori_loop(0, 8, one, (zero, zero))
+        put_row(ex.mine(e), 0, jnp.sum(acc[0], axis=0, keepdims=True))
+        put_row(ex.mine(e), 8, jnp.sum(acc[1], axis=0, keepdims=True))
+
+    def grad_rows(src, stats, k, d_of, sums, j):
+        hat = zhat(src, j, stats)
+        m = jnp.concatenate([mask[...]] * 5, axis=1)
+        got = passed(hat, k, d_of(j))
+        return (gain(k) * stats[1]) * (got - m * (sums[0] + hat * sums[1]) / valid_count)
+
+    def head_rows(j):
+        return jnp.concatenate([d_out24] * 8, axis=0)
+
+    def turn(src):
+        for it in range(4):
+            x = src[384 * it : 384 * it + 384, :].T.astype(bf16)
+            for f in range(NF):
+                dyT[f // 2, f % 2, :, 384 * it : 384 * it + 384] = x[80 * f : 80 * f + 80]
+
+    trade = remote(dyT.at[:, 1 - p.c], dyS, us, ur, p.b, p.sib)
+
+    grad_sums(block_rows, stats2, 2, head_rows, 3)
+    slot = ex.mine(3)
+    slot[5:6, :] = jnp.full((1, 128), loss_part, f32)
+    slot[6:7, :] = jnp.concatenate([g_bias, jnp.zeros((1, 112), f32)], axis=1)
+    ex.send(3)
+    tot3 = ex.total(3)
+    sums2 = wide(tot3[0:5]), wide(tot3[8:13])
+
+    def low_sums(dst, src, stats, k, d_of, sums):
+        def one(j, acc):
+            d = grad_rows(src, stats, k, d_of, sums, j)
+            dst[rows(j), :] = d
+            return acc + jnp.sum(d.astype(bf16).astype(f32).reshape(BLK // 8, 8, C), axis=0)
+
+        acc = lax.fori_loop(0, 8, one, jnp.zeros((8, C), f32))
+        return jnp.sum(acc, axis=0, keepdims=True)
+
+    def lost(dy_sums, mu):
+        at = 64 * p.b + iota((64, C), 0)
+        o = at - 80 * ((at >= 80).astype(jnp.int32) + (at >= 160).astype(jnp.int32))
+        hit = (iota((64, C), 1) == 80 * p.f + o) & (at < 240)
+        return jnp.sum(jnp.where(hit, dy_sums, 0.0), axis=1, keepdims=True) * mu
+
+    put_spare(ex.mine(4), low_sums(block, block_rows, stats2, 2, head_rows, sums2))
+    turn(block)
+    trade.start()
+    for u in range(3):
+        share(u).wait()
+    trade.wait()
+    filter_grad(p, S, S2, dyT, dyS, DS, mu1, G, 0)
+    sc.begin(0)
+    filter_grad(p, S, S2, dyT, dyS, DS, mu1, G, 1)
+    sc.begin(1)
+    filter_grad(p, S, S2, dyT, dyS, DS, mu1, G, 2)
+    sc.begin(2)
+    sc.mid(0)
+    pl.semaphore_signal(free, inc=1, device_id=(p.b, p.sib), device_id_type=MESH)
+
+    def spread(src):
+        def one(j, carry):
+            spread_rows(S, j, src[rows(j), :])
+            return carry
+
+        lax.fori_loop(0, 8, one, 0)
+
+    spread(block)
+
+    def back_conv1(it, carry):
+        r0 = pl.multiple_of(it * 384, 384)
+        dfl[pl.ds(r0, 384), :] = conv_back_rows(S, W, 1, r0, 384)
+
+        @pl.when(it == 1)
+        def _():
+            sc.mid(1)
+
+        @pl.when(it == 3)
+        def _():
+            sc.mid(2)
+
+        return carry
+
+    lax.fori_loop(0, 4, back_conv1, 0)
+    grad_sums(inner_rows, stats1, 1, dfl_rows, 4)
+    ex.send(4)
+    normed(base_rows, stats0, 0)
+    pl.semaphore_wait(free, 1)
+    for u in range(3):
+        share(u).start()
+    sc.along(0)
+    tot4 = ex.total(4)
+    sums1 = wide(tot4[0:5]), wide(tot4[8:13])
+    lost1 = lost(spare(tot4), mu1)
+    put_spare(ex.mine(5), low_sums(dfl, inner_rows, stats1, 1, dfl_rows, sums1))
+    turn(dfl)
+    trade.start()
+    sc.along(1)
+    sc.along(2)
+    sc.clear(0)
+    share(0).wait()
+    trade.wait()
+    filter_grad(p, S, S2, dyT, dyS, DS, mu0, G, 3)
+    sc.begin(3)
+    squares = sc.final(0, lost1)
+    sc.clear(1)
+    share(1).wait()
+    filter_grad(p, S, S2, dyT, dyS, DS, mu0, G, 4)
+    sc.begin(4)
+    squares = squares + sc.final(1, lost1)
+    sc.clear(2)
+    share(2).wait()
+    filter_grad(p, S, S2, dyT, dyS, DS, mu0, G, 5)
+    sc.begin(5)
+    squares = squares + sc.final(2, lost1)
+    sc.mid(3)
+    spread(dfl)
+
+    def back_conv0(it, carry):
+        r0 = pl.multiple_of(it * 384, 384)
+        inner[pl.ds(r0, 384), :] = conv_back_rows(S, W, 0, r0, 384)
+
+        @pl.when(it == 2)
+        def _():
+            sc.mid(4)
+
+        return carry
+
+    lax.fori_loop(0, 4, back_conv0, 0)
+
+    grad_sums(base_rows, stats0, 0, inner_rows, 5)
+    ex.send(5)
+    sc.mid(5)
+    sc.along(3)
+    sc.along(4)
+    tot5 = ex.total(5)
+    lost0 = lost(spare(tot5), mu0)
+    sums0 = wide(tot5[0:5]), wide(tot5[8:13])
+    grid16 = dfl.at[512:640]
+    grid16[...] = jnp.zeros((128, C), f32)
+    dstem[...] = jnp.zeros((BLK, 128), f32)
+
+    def back0(j, carry):
+        d = block[rows(j), :] + grad_rows(base_rows, stats0, 0, inner_rows, sums0, j)
+        d = d.astype(bf16)
+        pick = iota((BLK, 128), 1) // 16 == j
+        x = jnp.where(pick, stem[...], 0.0).astype(bf16)
+        grid16[...] += lax.dot_general(x, d, CC, preferred_element_type=f32)
+        y = lax.dot_general(d, bridge8, AC, preferred_element_type=f32)
+        dstem[...] += jnp.where(pick, y, 0.0)
+        return carry
+
+    lax.fori_loop(0, 8, back0, 0)
+    acc = grid16[0:16, :]
+    for j in range(1, 8):
+        acc = acc + grid16[16 * j : 16 * j + 16, :]
+    dfl[0:16, :] = acc
+    dfl[16:32, :] = par[24:40, :]
+
+    def half(row, c):
+        return dfl.at[pl.ds(pl.multiple_of(row + 16 * c, 16), 16), :]
+
+    give = remote(half(0, 1 - p.c), half(32, 1 - p.c), fs, fr, p.b, p.sib)
+    give.start()
+    sc.along(5)
+    low = dstem[...].astype(bf16)
+    high = lax.Precision.HIGHEST
+    acc = None
+    for c in range(3):
+        t = lax.dot_general(
+            AB[:, 128 * c : 128 * c + 128].astype(bf16), low, CC, preferred_element_type=f32
+        )
+        d = lax.dot_general(hits(c), t, CC, precision=high, preferred_element_type=f32)
+        acc = d if acc is None else acc + d
+    acc = jnp.where(own_j, acc, 0.0)
+    fold = (jnp.bitwise_and(iota((256, 128), 0), 31) == iota((256, 128), 1)).astype(f32)
+    acc = lax.dot_general(acc, fold, CC, precision=high, preferred_element_type=f32)
+    slots[6, p.chip] = jnp.dot(
+        tile_c.astype(f32), acc, precision=high, preferred_element_type=f32
+    )
+    ex.send(6)
+    squares = squares + sc.final(3, lost0)
+    give.wait()
+    zline = dfl.at[pl.ds(pl.multiple_of(64 + 16 * p.z, 16), 16), :]
+    zline[...] = half(0, p.c)[...] + half(32, p.c)[...]
+    for i in range(1, NZ):
+        to = lax.rem(p.z + i, NZ)
+        remote(zline, zline, hs, hr, p.b, 2 * to + p.c).start()
+    squares = squares + sc.final(4, lost0)
+    rest = dfl.at[64 : 64 + 16 * (NZ - 1), :]
+    remote(rest, rest, hs, hr, p.b, p.sib).wait()
+    square = dfl.at[pl.ds(pl.multiple_of(128 + 16 * p.b, 16), 16), :]
+    square[...] = jnp.sum(dfl[64:128, :].reshape(NZ, 16, C), axis=0)
+    for i in range(1, NB):
+        to = lax.rem(p.b + i, NB)
+        remote(square, square, js, jr, to, p.f).start()
+    g_stem = ex.total(6)
+    squares = squares + sc.final(5, lost0)
+    slots[7, p.chip] = jnp.full((16, 128), jnp.sum(squares), f32)
+    ex.send(7)
+    rest = dfl.at[128 : 128 + 16 * (NB - 1), :]
+    remote(rest, rest, js, jr, p.b, p.sib).wait()
+    done = half(192, p.c)
+    done[...] = jnp.sum(dfl[128:192, :].reshape(NB, 16, C), axis=0)
+    give = remote(done, done, ms, mr, p.b, p.sib)
+    give.start()
+    give.wait()
+    both = dfl[192:224, :]
+    bias_all = tot3[6:7, :]
+    bh_o[...] = both
+    small_o[...] = g_stem
+    norm_o[...] = jnp.zeros((8, C), f32)
+    for k, sums in enumerate((sums0, sums1, sums2)):
+        norm_o[2 * k : 2 * k + 1, :] = sums[1]
+        norm_o[2 * k + 1 : 2 * k + 2, :] = sums[0]
+    ng = norm_o[...]
+    other = jnp.sum(both * both) + jnp.sum(g_stem * g_stem) + jnp.sum(bias_all * bias_all)
+    other = other + jnp.sum(ng * ng)
+    conv_sq = ex.total(7)[0:1, :]
+    misc_o[...] = jnp.zeros((8, 128), f32)
+    misc_o[0:1, :] = jnp.sqrt(conv_sq + other)
+    misc_o[1:2, :] = tot3[5:6, :] / total
+    misc_o[2:3, :] = bias_all
+    for e in range(6):
+        sc.end(e)
+    for e in range(3, 6):
+        sc.clear(e)
+
+
+def step_call(images, labels, partner, valid, sizes, stem_w, bridge_t, conv_w, norm, head, bias):
+    V, A, SM = pltpu.VMEM, pl.ANY, pltpu.SMEM
+    spec = lambda m: pl.BlockSpec(memory_space=m)
+    D = pltpu.SemaphoreType.DMA
+    sh = jax.ShapeDtypeStruct
+    return pl.pallas_call(
+        step_kernel,
+        out_shape=(
+            sh((2, 3, 256, C), bf16), sh((32, C), f32), sh((16, 128), f32), sh((8, C), f32), sh((8, 128), f32),
+        ),
+        in_specs=[
+            spec(V), spec(V), spec(V), spec(V), spec(SM), spec(V), spec(V), spec(A), spec(V), spec(V), spec(V),
+        ],
+        out_specs=(spec(V),) * 5,
+        scratch_shapes=[
+            V((2, 3, NZ, 2, 256, C), bf16), V((3, 10 * BLK, C), bf16), V((3, 10 * BLK, C), bf16),
+            V((NZ, 2, 80, ROWS), bf16), V((NZ, 80, ROWS), bf16), V((NZ * 80, 128), f32),
+            V((ROWS, C), f32), V((ROWS, C), f32), V((ROWS, C), f32),
+            V((3, 3, 256, C), bf16), V((6, 3, 64, C), LINE), V((3, NZ, 256, C), bf16), V((3, NZ, 64, C), LINE),
+            V((8, NCHIP, 16, 128), f32), V((8, 2, 16, 128), f32), V((2, NCHIP, 128), f32), V((NF, 40, 128), f32), V((40, C), f32),
+            V((BLK, 128), f32), V((BLK, 384), f32), V((BLK, 128), f32), V((BLK, 128), f32), V((8, 128), f32),
+            D((8,)), D((8,)), D((8,)), D((8,)), D, D, D, D, D((6, 4)), D((6, 4)), D((6, 12)), D((6, 12)), D((6,)), D((6,)), D((1,)),
+            D((6, 6)), D((6, 6)), D((6, 3)), D((6, 3)), D((6, 3)), D((6, 3)), D((3,)), D((3,)), D, D,
+            pltpu.SemaphoreType.REGULAR, D, D, D, D, D, D, D, D,
+        ],
+        compiler_params=pltpu.CompilerParams(
+            collective_id=0, has_side_effects=True, vmem_limit_bytes=63 << 20
+        ),
+    )(images, labels, partner, valid, sizes, stem_w, bridge_t, conv_w, norm, head, bias)
 
 
 def make_patches(images):
@@ -321,6 +1245,55 @@
     )
 
 
+def fast_body(
+    images, labels, partner, valid_mask, group_sizes, stem_weight, bridge_weight, conv_weight, norm_params,
+    head_weight, head_bias, stem_first, stem_second, bridge_first, bridge_second, conv_first, conv_second,
+    norm_first, norm_second, head_first, head_second, bias_first, bias_second,
+):
+    width = bridge_weight.shape[0]
+    conv_grad, both, g_stem, g_norm, misc = step_call(
+        images, labels[None], partner[None], valid_mask[None], group_sizes, stem_weight, bridge_weight.T,
+        conv_weight.transpose(0, 2, 1, 3), norm_params, head_weight, head_bias[None],
+    )
+    conv_grad = conv_grad[:, :, :240].reshape(2, 9, width, C).transpose(0, 2, 1, 3).astype(f32)
+    both = lax.dynamic_slice_in_dim(both, lax.axis_index("filt") * width, width, 1)
+    bridge_sum, head_sum = both[:16].T, both[16:26]
+    norm_grad = lax.dynamic_slice_in_dim(g_norm[:6], lax.axis_index("filt") * width, width, 1)
+    stem_sum, bias_sum = g_stem[:, :27], misc[2, :10]
+    grad_norm, loss = misc[0, 0], misc[1, 0]
+    factor = clip_norm / jnp.maximum(grad_norm, clip_norm)
+    stem_new = adam_step(stem_weight, stem_sum, stem_first, stem_second, 0.5, 0.05, factor)
+    bridge_new = adam_step(
+        bridge_weight, bridge_sum, bridge_first, bridge_second, 0.6, 0.05, factor
+    )
+    conv_new = adam_step(conv_weight, conv_grad, conv_first, conv_second, 0.033, 0.05, factor)
+    norm_new = adam_step(norm_params, norm_grad, norm_first, norm_second, 0.5, 0.0, factor)
+    head_new = adam_step(head_weight, head_sum, head_first, head_second, 0.1, 0.05, factor)
+    bias_new = adam_step(head_bias, bias_sum, bias_first, bias_second, 0.5, 0.0, factor)
+    return (
+        stem_new[0],
+        stem_new[1],
+        stem_new[2],
+        bridge_new[0],
+        bridge_new[1],
+        bridge_new[2],
+        conv_new[0],
+        conv_new[1],
+        conv_new[2],
+        norm_new[0],
+        norm_new[1],
+        norm_new[2],
+        head_new[0],
+        head_new[1],
+        head_new[2],
+        bias_new[0],
+        bias_new[1],
+        bias_new[2],
+        grad_norm,
+        loss,
+    )
+
+
 def solution(mesh):
     in_specs = (
         P(("batch", "filt"), None),
@@ -369,4 +1342,5 @@
         P(),
         P(),
     )
-    return jax.shard_map(body, mesh=mesh, in_specs=in_specs, out_specs=out_specs, check_vma=False)
+    fits = mesh.shape["batch"] == NB and mesh.shape["filt"] == NF
+    return jax.shard_map(fast_body if fits else body, mesh=mesh, in_specs=in_specs, out_specs=out_specs, check_vma=False)

time: 1190 us -> 283 us (0.24)
  blocking collectives: 520 us -> 0 us
  Pallas kernels: 0 us -> 264 us
  waiting for transfers between devices: 247 us -> 0 us
  local copies, waits for them, and re-layouts: 146 us -> 1.35 us
  matrix products: 129 us -> 0 us
  other arithmetic: 113 us -> 15.2 us
  between operations: 25.1 us -> 1.58 us
    psum x12 -> x0, blocking collectives: 433 us -> none  [the longest x3 124 us: norm_forward(): lax.psum(jnp.sum(centered_input * centered_input * row_validity_mask, axi...]
    pallas_call x0 -> x1, Pallas kernels: none -> 264 us  [step_call(): pl.pallas_call(step_kernel, out_shape=(sh((2, 3, 256, C), bf16), sh((32,...]
    reduce_scatter x2 -> x0, waiting for transfers between devices: 148 us -> none  [conv_backward(): lax.psum_scatter(term.reshape(lax.axis_size('filt') * weight_shard.shape[...]
    dot_general x11 -> x0, matrix products: 126 us -> none  [the longest x2 45.5 us: conv_backward(): lax.dot_general(piece.reshape(piece.shape[0], -1), rows_grad, (((0,), (0,...]
    psum x1 -> x0, waiting for transfers between devices: 86.8 us -> none  [body(): lax.psum((jnp.stack([conv_grad_zero, conv_grad_one]), bridge_part, head_p...]
    slice x15 -> x1, local copies, waits for them, and re-layouts: 60.3 us -> 1.27 us  [fast_body(): grad_norm, loss = (misc[0, 0], misc[1, 0])]
    unnamed x168 -> x34, local copies, waits for them, and re-layouts: 52.5 us -> 0.08 us
    all_gather x3 -> x0, blocking collectives: 46 us -> none  [the longest x1 16.1 us: body(): lax.all_gather(head_weight, 'filt', axis=1, tiled=True)]
  transfers between devices with their start and end apart: 7 -> 0, of which waited for: 3 -> 0; matrix products, arithmetic and copies ran while one was open for 18% -> 0% of each run, Pallas kernels for 0% -> 0%
where the time goes in v1:
time: 283 us; the launch traced here: 282 us
  Pallas kernels  264 us (93%)
  other arithmetic  15.2 us (5%)
    pallas_call x1, Pallas kernels, step_call(): pl.pallas_call(step_kernel, out_shape=(sh((2, 3, 256, C), bf16), sh((32,...  264 us
    sub x6, other arithmetic, adam_step(): weight - rate * (ahead / (jnp.sqrt(behind) + adam_eps) + shrink * weight)  13.4 us

profile of v1, /device:TPU:1, one launch (start us, length us, event | category | flops | bytes accessed | tf_op | source)
XLA Modules:
  0.0 282.3 jit_solution(11735648522584376762)
XLA Ops:
  0.7 0.0 copy-start.2
  0.7 0.0 copy-start.14
  0.7 0.0 copy-start.4
  0.7 0.0 copy-start.1
  0.7 0.0 copy-start.5
  0.7 0.0 copy-start.6
  0.7 0.0 copy-start.7
  0.7 0.0 copy-start.8
  0.7 0.0 copy-start.12
  0.8 0.0 copy-start.13
  0.8 0.0 copy-start.15
  0.8 0.0 copy-start.16
  0.8 264.2 %shard_map.374 = (bf16[2,3,256,640]{3,2,1,0:T(8,128)(2,1)}, f32[32,640]{1,0:T(8,128)}, f32[16,128]{1,0:T(8,128)}, f32[8,640]{1,0:T(8,128)}, f32[8,128]{1,0:T(8,128)}) custom-call(bf16[24,3072]{1,0:T(8,128)(2,1)} %images.1, s32[1,24]{1,0:T(1,128)} %bitcast.32, s32[1,24]{1,0:T(1,128)} %bitcast.33, s32[1,24]{1,0:T(1,128)} %bitcast.34, s32[4,8]{1,0:T(4,128)} %sizes.1, ...), custom_call_target="tpu_custom_call" | custom-call | tf_op jit(solution)/shard_map/pallas_call | solution.py:915
  265.0 1.3 fusion.15
  266.9 0.0 copy-done.1
  266.9 0.0 copy-done.5
  267.0 0.0 copy-done.6
  267.0 0.0 copy-start
  267.0 1.6 multiply_subtract_fusion.1
  268.6 0.0 copy-done.2
  268.6 0.0 copy-done.7
  268.6 1.4 multiply_subtract_fusion.2
  270.0 0.0 copy-done.12
  270.0 1.4 multiply_subtract_fusion.4
  271.4 0.0 copy-done.14
  271.4 1.2 multiply_subtract_fusion.5
  272.6 1.7 convert_multiply_fusion
  274.4 0.0 copy-start.3
  274.4 0.0 copy-start.9
  274.4 0.0 copy-start.10
  274.4 7.2 %multiply_subtract_fusion = (f32[2,80,9,640]{3,1,2,0:T(8,128)}, f32[2,80,9,640]{3,1,2,0:T(8,128)}, f32[2,80,9,640]{3,1,2,0:T(8,128)}) fusion(f32[2,80,9,640]{3,1,2,0:T(8,128)S(1)} %copy-done, f32[2,80,9,640]{3,1,2,0:T(8,128)S(1)} %bitcast.28, f32[2,80,9,640]{3,1,2,0:T(8,128)} %param.38, f32[2,80,9,640]{3,1,2,0:T(8,128)} %param.39), kind=kLoop, calls=%fused_computation.2 | loop fusion | flops 13824000 | bytes 25804800 | tf_op jit(solution)/shard_map/sub | solution.py:1077
  281.6 0.6 multiply_subtract_fusion.3
  (11 shorter events, 0.0 us)
Async XLA Ops:
  0.7 267.9 %copy-start.2 = (f32[80,16]{0,1:T(8,128)S(1)}, f32[80,16]{0,1:T(8,128)}, u32[]{:S(2)}) copy-start(f32[80,16]{0,1:T(8,128)} %param.29) | copy-start | bytes 15364
  0.7 270.7 %copy-start.14 = (f32[10]{0:T(128)S(1)}, f32[10]{0:T(128)}, u32[]{:S(2)}) copy-start(f32[10]{0:T(128)} %param.33) | copy-start | bytes 124
  0.7 269.3 %copy-start.4 = (f32[6,80]{1,0:T(8,128)S(1)}, f32[6,80]{1,0:T(8,128)}, u32[]{:S(2)}) copy-start(f32[6,80]{1,0:T(8,128)} %norm.1) | copy-start | bytes 5764
  0.7 266.2 %copy-start.1 = (f32[10,80]{1,0:T(8,128)S(1)}, f32[10,80]{1,0:T(8,128)}, u32[]{:S(2)}) copy-start(f32[10,80]{1,0:T(8,128)} %head.1) | copy-start | bytes 9604
  0.7 266.2 %copy-start.5 = (f32[10,80]{1,0:T(8,128)S(1)}, f32[10,80]{1,0:T(8,128)}, u32[]{:S(2)}) copy-start(f32[10,80]{1,0:T(8,128)} %param.42) | copy-start | bytes 9604
  0.7 266.2 %copy-start.6 = (f32[10,80]{1,0:T(8,128)S(1)}, f32[10,80]{1,0:T(8,128)}, u32[]{:S(2)}) copy-start(f32[10,80]{1,0:T(8,128)} %param.43) | copy-start | bytes 9604
  0.7 267.8 %copy-start.7 = (f32[80,16]{0,1:T(8,128)S(1)}, f32[80,16]{0,1:T(8,128)}, u32[]{:S(2)}) copy-start(f32[80,16]{0,1:T(8,128)} %param.36) | copy-start | bytes 15364
  0.7 267.8 %copy-start.8 = (f32[80,16]{0,1:T(8,128)S(1)}, f32[80,16]{0,1:T(8,128)}, u32[]{:S(2)}) copy-start(f32[80,16]{0,1:T(8,128)} %param.37) | copy-start | bytes 15364
  0.7 269.3 %copy-start.12 = (f32[6,80]{1,0:T(8,128)S(1)}, f32[6,80]{1,0:T(8,128)}, u32[]{:S(2)}) copy-start(f32[6,80]{1,0:T(8,128)} %param.40) | copy-start | bytes 5764
  0.8 269.2 %copy-start.13 = (f32[6,80]{1,0:T(8,128)S(1)}, f32[6,80]{1,0:T(8,128)}, u32[]{:S(2)}) copy-start(f32[6,80]{1,0:T(8,128)} %param.41) | copy-start | bytes 5764
  0.8 270.6 %copy-start.15 = (f32[10]{0:T(128)S(1)}, f32[10]{0:T(128)}, u32[]{:S(2)}) copy-start(f32[10]{0:T(128)} %param.44) | copy-start | bytes 124
  0.8 270.6 %copy-start.16 = (f32[10]{0:T(128)S(1)}, f32[10]{0:T(128)}, u32[]{:S(2)}) copy-start(f32[10]{0:T(128)} %param.45) | copy-start | bytes 124
  267.0 7.4 %copy-start = (f32[2,80,9,640]{3,1,2,0:T(8,128)S(1)}, f32[2,80,9,640]{3,1,2,0:T(8,128)}, u32[]{:S(2)}) copy-start(f32[2,80,9,640]{3,1,2,0:T(8,128)} %param.30) | copy-start | bytes 11059204
  274.4 7.2 %copy-start.3 = (f32[16,27]{1,0:T(8,128)S(1)}, f32[16,27]{1,0:T(8,128)}, u32[]{:S(2)}) copy-start(f32[16,27]{1,0:T(8,128)} %stem_w.1) | copy-start | bytes 5188
  274.4 7.2 %copy-start.9 = (f32[16,27]{1,0:T(8,128)S(1)}, f32[16,27]{1,0:T(8,128)}, u32[]{:S(2)}) copy-start(f32[16,27]{1,0:T(8,128)} %param.34) | copy-start | bytes 5188
  274.4 7.2 %copy-start.10 = (f32[16,27]{1,0:T(8,128)S(1)}, f32[16,27]{1,0:T(8,128)}, u32[]{:S(2)}) copy-start(f32[16,27]{1,0:T(8,128)} %param.35) | copy-start | bytes 5188
  274.4 7.2 %copy-start.11 = (f32[16,128]{1,0:T(8,128)S(1)}, f32[16,128]{1,0:T(8,128)}, u32[]{:S(2)}) copy-start(f32[16,128]{1,0:T(8,128)} %get-tuple-element.25) | copy-start | bytes 24580

commit v2 on v1

--- a/solution.py
+++ b/solution.py
@@ -58,21 +58,22 @@
     )
 
 
+def peers(p):
+    for dz in (2, 1, 3, 0):
+        for db in (3, 1, 2, 0):
+            if dz or db:
+                yield lax.rem(p.b + db, NB), lax.rem(p.z + dz, NZ)
+
+
 def greet(p):
     sem = pltpu.get_barrier_semaphore()
-
-    def hello(i, carry):
-        to = lax.rem(p.me + i, NDEV)
-        pl.semaphore_signal(
-            sem, inc=1, device_id=(to // NF, lax.rem(to, NF)), device_id_type=MESH
-        )
-        return carry
-
-    lax.fori_loop(1, NDEV, hello, 0)
+    for b, z in peers(p):
+        pl.semaphore_signal(sem, inc=1, device_id=(b, 2 * z + p.c), device_id_type=MESH)
+    pl.semaphore_signal(sem, inc=1, device_id=(p.b, p.sib), device_id_type=MESH)
 
 
 def met():
-    pl.semaphore_wait(pltpu.get_barrier_semaphore(), NDEV - 1)
+    pl.semaphore_wait(pltpu.get_barrier_semaphore(), NCHIP)
 
 
 class Exchange:
@@ -86,30 +87,32 @@
     def send(self, e):
         p = self.p
         mine = self.mine(e)
-
-        def one(i, carry):
-            to = lax.rem(p.chip + i, NCHIP)
-            remote(
-                mine, mine, self.ssem.at[e], self.rsem.at[e], to // NZ, 2 * lax.rem(to, NZ) + p.c
-            ).start()
-            return carry
-
-        lax.fori_loop(1, NCHIP, one, 0)
-
-    def wait(self, e):
+        for b, z in peers(p):
+            remote(mine, mine, self.ssem.at[e], self.rsem.at[e], b, 2 * z + p.c).start()
+
+    def rest(self, e):
         p = self.p
         rest = self.slots.at[e, 0 : NCHIP - 1]
-        remote(rest, rest, self.ssem.at[e], self.rsem.at[e], p.b, p.sib).wait()
-
-    def swap(self, e, value):
+        return remote(rest, rest, self.ssem.at[e], self.rsem.at[e], p.b, p.sib)
+
+    def across(self, e):
         p = self.p
-        self.sibs[e, 0] = value
-        copy = remote(
+        return remote(
             self.sibs.at[e, 0], self.sibs.at[e, 1], self.psem.at[e], self.qsem.at[e], p.b, p.sib
         )
-        copy.start()
-        copy.wait()
+
+    def wait(self, e):
+        self.rest(e).wait_recv()
+
+    def swap(self, e, value):
+        self.sibs[e, 0] = value
+        self.across(e).start()
+        self.across(e).wait_recv()
         return self.sibs[e, 1]
+
+    def drain(self, e):
+        self.rest(e).wait_send()
+        self.across(e).wait_send()
 
     def total(self, e):
         self.wait(e)
@@ -181,22 +184,18 @@
     S[2, at, :] = jnp.concatenate([x[IMG:], gap], axis=0).astype(bf16)
 
 
-def conv_rows(S, W, k, r0, M):
-    acc = None
-    for u in range(3):
-        lhs = jnp.concatenate([S[u, pl.ds(r0 + v * BLK, M), :] for v in range(3)], axis=1)
-        rhs = jnp.concatenate(
-            [
-                jnp.concatenate(
-                    [W[k, u, z, c, v * 80 : v * 80 + 80, :] for z in range(NZ) for c in range(2)], axis=0
-                )
-                for v in range(3)
-            ],
-            axis=1,
-        )
-        d = lax.dot_general(lhs, rhs, AC, preferred_element_type=f32)
-        acc = d if acc is None else acc + d
-    return acc
+def conv_part(S, W, k, u, r0, M):
+    lhs = jnp.concatenate([S[u, pl.ds(r0 + v * BLK, M), :] for v in range(3)], axis=1)
+    rhs = jnp.concatenate(
+        [
+            jnp.concatenate(
+                [W[k, u, z, c, v * 80 : v * 80 + 80, :] for z in range(NZ) for c in range(2)], axis=0
+            )
+            for v in range(3)
+        ],
+        axis=1,
+    )
+    return lax.dot_general(lhs, rhs, AC, preferred_element_type=f32)
 
 
 class Gather:
@@ -369,22 +368,40 @@
     return acc
 
 
-def filter_grad(p, S, S2, dyT, dyS, DS, mu, G, e):
+def own_rows(p, dyT):
+    return jnp.concatenate([dyT[z, p.c] for z in range(NZ)], axis=0)
+
+
+def sib_rows(dyS):
+    return jnp.concatenate([dyS[z] for z in range(NZ)], axis=0)
+
+
+def first_grad(p, S, dyT, acc):
+    def tap(v, carry):
+        at = pl.ds(pl.multiple_of(v * BLK, BLK), ROWS)
+        acc[pl.ds(pl.multiple_of(v * 320, 320), 320), :] = jnp.dot(
+            own_rows(p, dyT), S[0, at, :], preferred_element_type=f32
+        )
+        return carry
+
+    lax.fori_loop(0, 3, tap, 0)
+
+
+def filter_grad(p, S, S2, dyT, dyS, DS, mu, G, e, acc):
     u = e % 3
     if u == 0:
         ones = jnp.ones((ROWS, 128), bf16)
-        own = jnp.concatenate([dyT[z, p.c] for z in range(NZ)], axis=0)
-        sib = jnp.concatenate([dyS[z] for z in range(NZ)], axis=0)
-        DS[...] = jnp.dot(own, ones, preferred_element_type=f32) + jnp.dot(
-            sib, ones, preferred_element_type=f32
+        DS[...] = jnp.dot(own_rows(p, dyT), ones, preferred_element_type=f32) + jnp.dot(
+            sib_rows(dyS), ones, preferred_element_type=f32
         )
 
     def tap(v, carry):
         at = pl.ds(pl.multiple_of(v * BLK, BLK), ROWS)
-        own = jnp.concatenate([dyT[z, p.c] for z in range(NZ)], axis=0)
-        sib = jnp.concatenate([dyS[z] for z in range(NZ)], axis=0)
-        d = jnp.dot(own, S[u, at, :], preferred_element_type=f32)
-        d = d + jnp.dot(sib, S2[u, at, :], preferred_element_type=f32)
+        d = jnp.dot(sib_rows(dyS), S2[u, at, :], preferred_element_type=f32)
+        if u == 0:
+            d = d + acc[pl.ds(pl.multiple_of(v * 320, 320), 320), :]
+        else:
+            d = d + jnp.dot(own_rows(p, dyT), S[u, at, :], preferred_element_type=f32)
         d = d - jnp.concatenate([DS[...]] * 5, axis=1) * mu
         for z in range(NZ):
             G[u, z, pl.ds(pl.multiple_of(v * 80, 16), 80), :] = d[80 * z : 80 * z + 80].astype(bf16)
@@ -395,7 +412,7 @@
 
 def step_kernel(
     images, labels, partner, valid, sizes, stem_w, bridge_t, conv_w, norm, head, bias,
-    GF, bh_o, small_o, norm_o, misc_o,
+    GF, own_o, stem_o, misc_o,
     W, S, S2, dyT, dyS, DS, inner, block, dfl, RX, RZ, G, Q, slots, sibs, lab, gath, par, mask, AB, stem, dstem, pad,
     xs_, xr_, ps_, pr_, lbs, lbr, gs, gr, zs, zr, xs, xr, ds, dr, ls,
     bs, br, cs, cr, es, er, ts, tr, us, ur, free, fs, fr, hs, hr, js, jr, ms, mr,
@@ -405,29 +422,31 @@
     ga = Gather(p, W, zs, zr, xs, xr, ds, dr)
     sc = Scatter(p, W, RX, RZ, G, Q, GF, (bs, br, cs, cr, es, er))
     greet(p)
-    load = pltpu.make_async_copy(conv_w.reshape(1440, C), block.at[pl.ds(0, 1440)], ls.at[0])
-    load.start()
-    mine = gath.at[p.f]
+    def load(s):
+        at = pl.ds(240 * s, 240)
+        return pltpu.make_async_copy(conv_w.reshape(1440, C).at[at], block.at[at], ls.at[s])
+
+    for s in range(6):
+        load(s).start()
+    mine = gath.at[p.z, p.c]
     mine[...] = jnp.zeros((40, 128), f32)
     mine[0:16, 0:80] = bridge_t[...]
     mine[16:22, 0:80] = norm[...]
     mine[24:34, 0:80] = head[...]
-    def small(i):
-        to = lax.rem(p.f + i, NF)
-        return remote(mine, mine, gs, gr, p.b, to)
 
     def cast(s):
+        load(s).wait()
         k, u = s // 3, s % 3
         for v in range(3):
             t = 9 * k + 3 * u + v
             W[k, u, p.z, p.c, 80 * v : 80 * v + 80, :] = block[80 * t : 80 * t + 80, :].astype(bf16)
         W[k, u, p.z, p.c, 240:256, :] = jnp.zeros((16, C), bf16)
 
-    load.wait()
     cast(0)
     met()
-    for i in range(1, NF):
-        small(i).start()
+    for i in (2, 1, 3):
+        to = lax.rem(p.z + i, NZ)
+        remote(mine, mine, gs.at[0], gr.at[0], p.b, 2 * to + p.c).start()
     ga.zsend(0)
     for s in range(1, 6):
         cast(s)
@@ -490,15 +509,19 @@
         S[u, 9 * BLK : 10 * BLK, :] = edge
         for z in range(NZ):
             G[u, z, 240:256, :] = jnp.zeros((16, C), bf16)
-    rest = gath.at[0 : NF - 1]
-    remote(rest, rest, gs, gr, p.b, p.sib).wait()
+    rest = gath.at[0 : NZ - 1, 0]
+    remote(rest, rest, gs.at[0], gr.at[0], p.b, p.sib).wait()
+    side = gath.at[:, p.c]
+    pair = remote(side, side, gs.at[1], gr.at[1], p.b, p.sib)
+    pair.start()
+    pair.wait()
     lane = iota((40, 128), 1)
     for k in range(5):
         acc = jnp.zeros((40, 128), f32)
         for f in range(NF):
             lo, hi = max(80 * f, 128 * k), min(80 * f + 80, 128 * k + 128)
             if lo < hi:
-                turned = pltpu.roll(gath[f], (80 * f - 128 * k) % 128, 1)
+                turned = pltpu.roll(gath[f // 2, f % 2], (80 * f - 128 * k) % 128, 1)
                 acc = jnp.where((lane >= lo - 128 * k) & (lane < hi - 128 * k), turned, acc)
         par[:, 128 * k : 128 * k + 128] = acc
     bridge8 = jnp.concatenate([par[0:16, :].astype(bf16)] * 8, axis=0)
@@ -557,61 +580,53 @@
     put_spare(ex.mine(1), normed(inner_rows, stats0, 0))
     for s in range(3, 6):
         ga.zsend(s)
+
+    def conv(k, u, dst, start, acts):
+        def one(it, carry):
+            r0 = pl.multiple_of(it * 384, 384)
+            at = pl.ds(r0, 384)
+            d = conv_part(S, W, k, u, r0, 384)
+            dst[at, :] = (dst[at, :] if start is None else start(it)) + d if start != 0 else d
+            for when, act in acts.items():
+                pl.when(it == when)(act)
+            return carry
+
+        lax.fori_loop(0, 4, one, 0)
+
+    def share(u):
+        return remote(S.at[u], S2.at[u], ts.at[u], tr.at[u], p.b, p.sib)
+
+    def doing(f, *a):
+        return lambda: f(*a)
+
     ga.relay(2)
     ga.turn(1)
     ga.across(0)
-    ga.turn(2)
-    ga.relay(3)
+    ga.arrive(0)
+    conv(0, 0, inner, 0, {0: doing(ga.turn, 2), 1: doing(ga.relay, 3)})
     ga.across(1)
+    ga.relay(4)
     ga.across(2)
-    ga.relay(4)
-    for s in range(3):
-        ga.arrive(s)
-
-    def conv0(it, carry):
-        r0 = pl.multiple_of(it * 384, 384)
-        inner[pl.ds(r0, 384), :] = conv_rows(S, W, 0, r0, 384)
-
-        @pl.when(it == 0)
-        def _():
-            ga.relay(5)
-
-        @pl.when(it == 1)
-        def _():
-            ga.turn(3)
-            ga.turn(4)
-
-        @pl.when(it == 3)
-        def _():
-            ga.turn(5)
-            ga.across(3)
-
-        return carry
-
-    lax.fori_loop(0, 4, conv0, 0)
+    ga.arrive(1)
+    conv(0, 1, inner, None, {})
+    ga.arrive(2)
+    conv(0, 2, inner, None, {0: doing(ga.turn, 3), 2: doing(ga.relay, 5)})
     local_stats(inner, mask, count, ex.mine(1))
     ex.send(1)
-    ga.across(4)
+    ga.turn(4)
+    ga.across(3)
     stats1 = joint_stats(ex, 1)
+    ga.turn(5)
     put_spare(ex.mine(2), normed(inner_rows, stats1, 1))
-    ga.across(5)
-    for s in range(3, 6):
-        ga.arrive(s)
-
-    def share(u):
-        return remote(S.at[u], S2.at[u], ts.at[u], tr.at[u], p.b, p.sib)
-
+    ga.arrive(3)
+    conv(1, 0, block, lambda it: jnp.concatenate([base_rows(2 * it), base_rows(2 * it + 1)], axis=0),
+         {1: doing(ga.across, 4), 3: doing(ga.across, 5)})
+    ga.arrive(4)
     for u in range(3):
         share(u).start()
-
-    def conv1(it, carry):
-        r0 = pl.multiple_of(it * 384, 384)
-        at = pl.ds(r0, 384)
-        low = jnp.concatenate([base_rows(2 * it), base_rows(2 * it + 1)], axis=0)
-        block[at, :] = low + conv_rows(S, W, 1, r0, 384)
-        return carry
-
-    lax.fori_loop(0, 4, conv1, 0)
+    conv(1, 1, block, None, {})
+    ga.arrive(5)
+    conv(1, 2, block, None, {})
     local_stats(block, mask, count, ex.mine(2))
     ex.send(2)
     for s in range(6):
@@ -726,16 +741,17 @@
     put_spare(ex.mine(4), low_sums(block, block_rows, stats2, 2, head_rows, sums2))
     turn(block)
     trade.start()
+    first_grad(p, S, dyT, dfl)
     for u in range(3):
         share(u).wait()
     trade.wait()
-    filter_grad(p, S, S2, dyT, dyS, DS, mu1, G, 0)
+    filter_grad(p, S, S2, dyT, dyS, DS, mu1, G, 0, dfl)
     sc.begin(0)
-    filter_grad(p, S, S2, dyT, dyS, DS, mu1, G, 1)
+    filter_grad(p, S, S2, dyT, dyS, DS, mu1, G, 1, dfl)
     sc.begin(1)
-    filter_grad(p, S, S2, dyT, dyS, DS, mu1, G, 2)
+    filter_grad(p, S, S2, dyT, dyS, DS, mu1, G, 2, dfl)
+    sc.mid(0)
     sc.begin(2)
-    sc.mid(0)
     pl.semaphore_signal(free, inc=1, device_id=(p.b, p.sib), device_id_type=MESH)
 
     def spread(src):
@@ -766,8 +782,7 @@
     ex.send(4)
     normed(base_rows, stats0, 0)
     pl.semaphore_wait(free, 1)
-    for u in range(3):
-        share(u).start()
+    share(0).start()
     sc.along(0)
     tot4 = ex.total(4)
     sums1 = wide(tot4[0:5]), wide(tot4[8:13])
@@ -775,34 +790,41 @@
     put_spare(ex.mine(5), low_sums(dfl, inner_rows, stats1, 1, dfl_rows, sums1))
     turn(dfl)
     trade.start()
+    for u in range(1, 3):
+        share(u).start()
     sc.along(1)
+    first_grad(p, S, dyT, inner)
     sc.along(2)
     sc.clear(0)
     share(0).wait()
     trade.wait()
-    filter_grad(p, S, S2, dyT, dyS, DS, mu0, G, 3)
+    filter_grad(p, S, S2, dyT, dyS, DS, mu0, G, 3, inner)
     sc.begin(3)
     squares = sc.final(0, lost1)
     sc.clear(1)
     share(1).wait()
-    filter_grad(p, S, S2, dyT, dyS, DS, mu0, G, 4)
+    filter_grad(p, S, S2, dyT, dyS, DS, mu0, G, 4, inner)
     sc.begin(4)
     squares = squares + sc.final(1, lost1)
     sc.clear(2)
     share(2).wait()
-    filter_grad(p, S, S2, dyT, dyS, DS, mu0, G, 5)
+    filter_grad(p, S, S2, dyT, dyS, DS, mu0, G, 5, inner)
+    sc.mid(3)
     sc.begin(5)
     squares = squares + sc.final(2, lost1)
-    sc.mid(3)
     spread(dfl)
 
     def back_conv0(it, carry):
         r0 = pl.multiple_of(it * 384, 384)
         inner[pl.ds(r0, 384), :] = conv_back_rows(S, W, 0, r0, 384)
 
+        @pl.when(it == 1)
+        def _():
+            sc.mid(4)
+
         @pl.when(it == 2)
         def _():
-            sc.mid(4)
+            sc.along(3)
 
         return carry
 
@@ -811,10 +833,10 @@
     grad_sums(base_rows, stats0, 0, inner_rows, 5)
     ex.send(5)
     sc.mid(5)
-    sc.along(3)
     sc.along(4)
     tot5 = ex.total(5)
     lost0 = lost(spare(tot5), mu0)
+    squares = squares + sc.final(3, lost0)
     sums0 = wide(tot5[0:5]), wide(tot5[8:13])
     grid16 = dfl.at[512:640]
     grid16[...] = jnp.zeros((128, C), f32)
@@ -859,7 +881,6 @@
         tile_c.astype(f32), acc, precision=high, preferred_element_type=f32
     )
     ex.send(6)
-    squares = squares + sc.final(3, lost0)
     give.wait()
     zline = dfl.at[pl.ds(pl.multiple_of(64 + 16 * p.z, 16), 16), :]
     zline[...] = half(0, p.c)[...] + half(32, p.c)[...]
@@ -887,15 +908,13 @@
     give.wait()
     both = dfl[192:224, :]
     bias_all = tot3[6:7, :]
-    bh_o[...] = both
-    small_o[...] = g_stem
-    norm_o[...] = jnp.zeros((8, C), f32)
-    for k, sums in enumerate((sums0, sums1, sums2)):
-        norm_o[2 * k : 2 * k + 1, :] = sums[1]
-        norm_o[2 * k + 1 : 2 * k + 2, :] = sums[0]
-    ng = norm_o[...]
-    other = jnp.sum(both * both) + jnp.sum(g_stem * g_stem) + jnp.sum(bias_all * bias_all)
-    other = other + jnp.sum(ng * ng)
+    stem_o[...] = g_stem
+    ng = [row for sums in (sums0, sums1, sums2) for row in (sums[1], sums[0])]
+    ng = jnp.concatenate(ng + [jnp.zeros((2, C), f32)], axis=0)
+    every = jnp.concatenate([both, ng], axis=0)
+    pick = (iota((C, 128), 0) == 80 * p.f + iota((C, 128), 1)) & (iota((C, 128), 1) < 80)
+    own_o[...] = jnp.dot(every, pick.astype(f32), precision=high, preferred_element_type=f32)
+    other = jnp.sum(every * every) + jnp.sum(g_stem * g_stem) + jnp.sum(bias_all * bias_all)
     conv_sq = ex.total(7)[0:1, :]
     misc_o[...] = jnp.zeros((8, 128), f32)
     misc_o[0:1, :] = jnp.sqrt(conv_sq + other)
@@ -905,6 +924,8 @@
         sc.end(e)
     for e in range(3, 6):
         sc.clear(e)
+    for e in range(8):
+        ex.drain(e)
 
 
 def step_call(images, labels, partner, valid, sizes, stem_w, bridge_t, conv_w, norm, head, bias):
@@ -915,20 +936,20 @@
     return pl.pallas_call(
         step_kernel,
         out_shape=(
-            sh((2, 3, 256, C), bf16), sh((32, C), f32), sh((16, 128), f32), sh((8, C), f32), sh((8, 128), f32),
+            sh((2, 3, 256, C), bf16), sh((40, 128), f32), sh((16, 128), f32), sh((8, 128), f32),
         ),
         in_specs=[
             spec(V), spec(V), spec(V), spec(V), spec(SM), spec(V), spec(V), spec(A), spec(V), spec(V), spec(V),
         ],
-        out_specs=(spec(V),) * 5,
+        out_specs=(spec(V),) * 4,
         scratch_shapes=[
             V((2, 3, NZ, 2, 256, C), bf16), V((3, 10 * BLK, C), bf16), V((3, 10 * BLK, C), bf16),
             V((NZ, 2, 80, ROWS), bf16), V((NZ, 80, ROWS), bf16), V((NZ * 80, 128), f32),
             V((ROWS, C), f32), V((ROWS, C), f32), V((ROWS, C), f32),
             V((3, 3, 256, C), bf16), V((6, 3, 64, C), LINE), V((3, NZ, 256, C), bf16), V((3, NZ, 64, C), LINE),
-            V((8, NCHIP, 16, 128), f32), V((8, 2, 16, 128), f32), V((2, NCHIP, 128), f32), V((NF, 40, 128), f32), V((40, C), f32),
+            V((8, NCHIP, 16, 128), f32), V((8, 2, 16, 128), f32), V((2, NCHIP, 128), f32), V((NZ, 2, 40, 128), f32), V((40, C), f32),
             V((BLK, 128), f32), V((BLK, 384), f32), V((BLK, 128), f32), V((BLK, 128), f32), V((8, 128), f32),
-            D((8,)), D((8,)), D((8,)), D((8,)), D, D, D, D, D((6, 4)), D((6, 4)), D((6, 12)), D((6, 12)), D((6,)), D((6,)), D((1,)),
+            D((8,)), D((8,)), D((8,)), D((8,)), D, D, D((2,)), D((2,)), D((6, 4)), D((6, 4)), D((6, 12)), D((6, 12)), D((6,)), D((6,)), D((6,)),
             D((6, 6)), D((6, 6)), D((6, 3)), D((6, 3)), D((6, 3)), D((6, 3)), D((3,)), D((3,)), D, D,
             pltpu.SemaphoreType.REGULAR, D, D, D, D, D, D, D, D,
         ],
@@ -936,6 +957,50 @@
             collective_id=0, has_side_effects=True, vmem_limit_bytes=63 << 20
         ),
     )(images, labels, partner, valid, sizes, stem_w, bridge_t, conv_w, norm, head, bias)
+
+
+def adam_rule(g, w, m, v, rate, shrink, factor):
+    clipped = g * factor
+    m = beta_one * m + (1.0 - beta_one) * clipped
+    v = beta_two * v + (1.0 - beta_two) * clipped * clipped
+    ahead = m / (1.0 - beta_one**STEP)
+    behind = v / (1.0 - beta_two**STEP)
+    return w - rate * (ahead / (jnp.sqrt(behind) + adam_eps) + shrink * w), m, v
+
+
+def adam_kernel(G, misc, own, stem_g, *refs):
+    ins, outs = refs[:18], refs[18:]
+    factor = clip_norm / jnp.maximum(misc[0:1, :], clip_norm)
+
+    def write(i, g, rate, shrink, f):
+        w, m, v = (r[...] for r in ins[3 * i : 3 * i + 3])
+        for o, x in zip(outs[3 * i : 3 * i + 3], adam_rule(g, w, m, v, rate, shrink, f)):
+            o[...] = x
+
+    g = G[0, 0, 0:240, :].astype(f32)
+    write(0, g[None, None], 0.033, 0.05, jnp.concatenate([factor] * 5, axis=1)[None, None])
+
+    @pl.when((pl.program_id(0) == 0) & (pl.program_id(1) == 0))
+    def _():
+        write(1, stem_g[:, 0:27], 0.5, 0.05, factor[:, 0:27])
+        write(2, own[0:16, 0:80], 0.6, 0.05, factor[:, 0:80])
+        write(3, own[32:38, 0:80], 0.5, 0.0, factor[:, 0:80])
+        write(4, own[16:26, 0:80], 0.1, 0.05, factor[:, 0:80])
+        write(5, misc[2:3, 0:10], 0.5, 0.0, factor[:, 0:10])
+
+
+def adam_call(G, misc, own, stem_g, *state):
+    whole = lambda x: pl.BlockSpec(x.shape, lambda k, u: (0,) * x.ndim)
+    tile = lambda n: pl.BlockSpec((1, 1, n, C), lambda k, u: (k, u, 0, 0))
+    specs = [tile(240)] * 3 + [whole(x) for x in state[3:]]
+    return pl.pallas_call(
+        adam_kernel,
+        out_shape=tuple(jax.ShapeDtypeStruct(x.shape, f32) for x in state),
+        grid=(2, 3),
+        in_specs=[tile(256), whole(misc), whole(own), whole(stem_g)] + specs,
+        out_specs=tuple(specs),
+        compiler_params=pltpu.CompilerParams(vmem_limit_bytes=62 << 20),
+    )(G, misc, own, stem_g, *state)
 
 
 def make_patches(images):
@@ -1251,46 +1316,35 @@
     norm_first, norm_second, head_first, head_second, bias_first, bias_second,
 ):
     width = bridge_weight.shape[0]
-    conv_grad, both, g_stem, g_norm, misc = step_call(
+    def rows(x):
+        return x.transpose(0, 2, 1, 3).reshape(2, 3, 3 * width, C)
+
+    def back(x):
+        return x.reshape(2, 9, width, C).transpose(0, 2, 1, 3)
+
+    G, own, stem_g, misc = step_call(
         images, labels[None], partner[None], valid_mask[None], group_sizes, stem_weight, bridge_weight.T,
         conv_weight.transpose(0, 2, 1, 3), norm_params, head_weight, head_bias[None],
     )
-    conv_grad = conv_grad[:, :, :240].reshape(2, 9, width, C).transpose(0, 2, 1, 3).astype(f32)
-    both = lax.dynamic_slice_in_dim(both, lax.axis_index("filt") * width, width, 1)
-    bridge_sum, head_sum = both[:16].T, both[16:26]
-    norm_grad = lax.dynamic_slice_in_dim(g_norm[:6], lax.axis_index("filt") * width, width, 1)
-    stem_sum, bias_sum = g_stem[:, :27], misc[2, :10]
-    grad_norm, loss = misc[0, 0], misc[1, 0]
-    factor = clip_norm / jnp.maximum(grad_norm, clip_norm)
-    stem_new = adam_step(stem_weight, stem_sum, stem_first, stem_second, 0.5, 0.05, factor)
-    bridge_new = adam_step(
-        bridge_weight, bridge_sum, bridge_first, bridge_second, 0.6, 0.05, factor
-    )
-    conv_new = adam_step(conv_weight, conv_grad, conv_first, conv_second, 0.033, 0.05, factor)
-    norm_new = adam_step(norm_params, norm_grad, norm_first, norm_second, 0.5, 0.0, factor)
-    head_new = adam_step(head_weight, head_sum, head_first, head_second, 0.1, 0.05, factor)
-    bias_new = adam_step(head_bias, bias_sum, bias_first, bias_second, 0.5, 0.0, factor)
+    new = adam_call(
+        G, misc, own, stem_g,
+        rows(conv_weight), rows(conv_first), rows(conv_second),
+        stem_weight, stem_first, stem_second,
+        bridge_weight.T, bridge_first.T, bridge_second.T,
+        norm_params, norm_first, norm_second,
+        head_weight, head_first, head_second,
+        head_bias[None], bias_first[None], bias_second[None],
+    )
+    conv, stem, bridge, norm, head, bias = (new[i : i + 3] for i in range(0, 18, 3))
     return (
-        stem_new[0],
-        stem_new[1],
-        stem_new[2],
-        bridge_new[0],
-        bridge_new[1],
-        bridge_new[2],
-        conv_new[0],
-        conv_new[1],
-        conv_new[2],
-        norm_new[0],
-        norm_new[1],
-        norm_new[2],
-        head_new[0],
-        head_new[1],
-        head_new[2],
-        bias_new[0],
-        bias_new[1],
-        bias_new[2],
-        grad_norm,
-        loss,
+        *stem,
+        *(x.T for x in bridge),
+        *(back(x) for x in conv),
+        *norm,
+        *head,
+        *(x[0] for x in bias),
+        misc[0, 0],
+        misc[1, 0],
     )
 
 

time: 283 us -> 259 us (0.915)
  other arithmetic: 15.2 us -> 0 us
  Pallas kernels: 264 us -> 257 us
    sub x6 -> x0, other arithmetic: 13.4 us -> none  [adam_step(): weight - rate * (ahead / (jnp.sqrt(behind) + adam_eps) + shrink * weight)]
    pallas_call x1 -> x2, Pallas kernels: 264 us -> 257 us  [the longest x1 245 us: step_call(): pl.pallas_call(step_kernel, out_shape=(sh((2, 3, 256, C), bf16), sh((40,...]
where the time goes in v2:
time: 259 us; the launch traced here: 258 us
  Pallas kernels  257 us (99%)
    pallas_call x1, Pallas kernels, step_call(): pl.pallas_call(step_kernel, out_shape=(sh((2, 3, 256, C), bf16), sh((40,...  245 us
    pallas_call x1, Pallas kernels, adam_call(): pl.pallas_call(adam_kernel, out_shape=tuple((jax.ShapeDtypeStruct(x.shape...  11.8 us

profile of v2, /device:TPU:1, one launch (start us, length us, event | category | flops | bytes accessed | tf_op | source)
XLA Modules:
  0.0 258.5 jit_solution(12085259692446238290)
XLA Ops:
  0.7 244.8 %shard_map.374 = (bf16[2,3,256,640]{3,2,1,0:T(8,128)(2,1)}, f32[40,128]{1,0:T(8,128)}, f32[16,128]{1,0:T(8,128)}, f32[8,128]{1,0:T(8,128)}) custom-call(bf16[24,3072]{1,0:T(8,128)(2,1)} %images.1, s32[1,24]{1,0:T(1,128)} %bitcast.47, s32[1,24]{1,0:T(1,128)} %bitcast.48, s32[1,24]{1,0:T(1,128)} %bitcast.49, s32[4,8]{1,0:T(4,128)} %sizes.1, f32[16,27]{1,0:T(8,128)} %refs_3_.1, ...), custom_call_target="tpu_custom_call" | custom-call | tf_op jit(solution)/shard_map/pallas_call | solution.py:936
  245.4 11.8 %shard_map.375 = (f32[2,3,240,640]{3,2,1,0:T(8,128)}, f32[2,3,240,640]{3,2,1,0:T(8,128)}, f32[2,3,240,640]{3,2,1,0:T(8,128)}, f32[16,27]{1,0:T(8,128)}, f32[16,2...) custom-call(bf16[2,3,256,640]{3,2,1,0:T(8,128)(2,1)} %get-tuple-elem, ...), custom_call_target="tpu_custom_call" | custom-call | tf_op jit(solution)/shard_map/pallas_call | solution.py:996
  257.2 1.3 fusion

commit v3 on v2

--- a/solution.py
+++ b/solution.py
@@ -179,13 +179,13 @@
 def spread_rows(S, j, x):
     at = pl.ds(pl.multiple_of((j + 1) * BLK, BLK), BLK)
     gap = jnp.zeros((IMG, C), f32)
-    S[0, at, :] = jnp.concatenate([gap, x[: BLK - IMG]], axis=0).astype(bf16)
-    S[1, at, :] = x.astype(bf16)
-    S[2, at, :] = jnp.concatenate([x[IMG:], gap], axis=0).astype(bf16)
+    S[0][at, :] = jnp.concatenate([gap, x[: BLK - IMG]], axis=0).astype(bf16)
+    S[1][at, :] = x.astype(bf16)
+    S[2][at, :] = jnp.concatenate([x[IMG:], gap], axis=0).astype(bf16)
 
 
 def conv_part(S, W, k, u, r0, M):
-    lhs = jnp.concatenate([S[u, pl.ds(r0 + v * BLK, M), :] for v in range(3)], axis=1)
+    lhs = jnp.concatenate([S[u][pl.ds(r0 + v * BLK, M), :] for v in range(3)], axis=1)
     rhs = jnp.concatenate(
         [
             jnp.concatenate(
@@ -342,6 +342,8 @@
     def clear(self, e):
         for i in range(6):
             self.hop(e, i).wait_send()
+
+    def clear_line(self, e):
         for i in range(1, NZ):
             self.out3(e, i).wait_send()
 
@@ -353,7 +355,7 @@
 def conv_back_rows(S, W, k, r0, M):
     acc = None
     for u in range(3):
-        lhs = jnp.concatenate([S[2 - u, pl.ds(r0 + (2 - v) * BLK, M), :] for v in range(3)], axis=1)
+        lhs = jnp.concatenate([S[2 - u][pl.ds(r0 + (2 - v) * BLK, M), :] for v in range(3)], axis=1)
         rhs = jnp.concatenate(
             [
                 W[k, u, z, c, v * 80 : v * 80 + 80, :]
@@ -380,7 +382,7 @@
     def tap(v, carry):
         at = pl.ds(pl.multiple_of(v * BLK, BLK), ROWS)
         acc[pl.ds(pl.multiple_of(v * 320, 320), 320), :] = jnp.dot(
-            own_rows(p, dyT), S[0, at, :], preferred_element_type=f32
+            own_rows(p, dyT), S[0][at, :], preferred_element_type=f32
         )
         return carry
 
@@ -401,7 +403,7 @@
         if u == 0:
             d = d + acc[pl.ds(pl.multiple_of(v * 320, 320), 320), :]
         else:
-            d = d + jnp.dot(own_rows(p, dyT), S[u, at, :], preferred_element_type=f32)
+            d = d + jnp.dot(own_rows(p, dyT), S[u][at, :], preferred_element_type=f32)
         d = d - jnp.concatenate([DS[...]] * 5, axis=1) * mu
         for z in range(NZ):
             G[u, z, pl.ds(pl.multiple_of(v * 80, 16), 80), :] = d[80 * z : 80 * z + 80].astype(bf16)
@@ -413,7 +415,7 @@
 def step_kernel(
     images, labels, partner, valid, sizes, stem_w, bridge_t, conv_w, norm, head, bias,
     GF, own_o, stem_o, misc_o,
-    W, S, S2, dyT, dyS, DS, inner, block, dfl, RX, RZ, G, Q, slots, sibs, lab, gath, par, mask, AB, stem, dstem, pad,
+    W, S, S2, S3, dyT, dyS, DS, inner, block, dfl, RX, RZ, G, Q, slots, sibs, lab, gath, par, mask, AB, stem, dstem, pad,
     xs_, xr_, ps_, pr_, lbs, lbr, gs, gr, zs, zr, xs, xr, ds, dr, ls,
     bs, br, cs, cr, es, er, ts, tr, us, ur, free, fs, fr, hs, hr, js, jr, ms, mr,
 ):
@@ -422,6 +424,8 @@
     ga = Gather(p, W, zs, zr, xs, xr, ds, dr)
     sc = Scatter(p, W, RX, RZ, G, Q, GF, (bs, br, cs, cr, es, er))
     greet(p)
+    SA = [S.at[u] for u in range(3)]
+    SB = [S.at[0], S.at[1], S3]
     def load(s):
         at = pl.ds(240 * s, 240)
         return pltpu.make_async_copy(conv_w.reshape(1440, C).at[at], block.at[at], ls.at[s])
@@ -504,6 +508,8 @@
     slot[6:7, :] = jnp.concatenate([own_row, jnp.zeros((1, 104), f32)], axis=1)
     slot[7:8, :] = jnp.full((1, 128), jnp.sum(weight), f32)
     edge = jnp.zeros((BLK, C), bf16)
+    S3[0:BLK, :] = edge
+    S3[9 * BLK : 10 * BLK, :] = edge
     for u in range(3):
         S[u, 0:BLK, :] = edge
         S[u, 9 * BLK : 10 * BLK, :] = edge
@@ -560,7 +566,7 @@
     def shift(k):
         return par[17 + 2 * k : 18 + 2 * k, :]
 
-    def normed(src, stats, k):
+    def normed(src, stats, k, S):
         mean, scale = stats[:2]
 
         def one(j, acc):
@@ -577,7 +583,7 @@
     labs = remote(lab.at[0], lab.at[1], lbs, lbr, p.b, p.sib)
     lab[0] = slots[0, :, 6, :]
     labs.start()
-    put_spare(ex.mine(1), normed(inner_rows, stats0, 0))
+    put_spare(ex.mine(1), normed(inner_rows, stats0, 0, SA))
     for s in range(3, 6):
         ga.zsend(s)
 
@@ -585,7 +591,7 @@
         def one(it, carry):
             r0 = pl.multiple_of(it * 384, 384)
             at = pl.ds(r0, 384)
-            d = conv_part(S, W, k, u, r0, 384)
+            d = conv_part(SB if k else SA, W, k, u, r0, 384)
             dst[at, :] = (dst[at, :] if start is None else start(it)) + d if start != 0 else d
             for when, act in acts.items():
                 pl.when(it == when)(act)
@@ -593,8 +599,8 @@
 
         lax.fori_loop(0, 4, one, 0)
 
-    def share(u):
-        return remote(S.at[u], S2.at[u], ts.at[u], tr.at[u], p.b, p.sib)
+    def share(u, S=SA):
+        return remote(S[u], S2.at[u], ts.at[u], tr.at[u], p.b, p.sib)
 
     def doing(f, *a):
         return lambda: f(*a)
@@ -605,25 +611,24 @@
     ga.arrive(0)
     conv(0, 0, inner, 0, {0: doing(ga.turn, 2), 1: doing(ga.relay, 3)})
     ga.across(1)
-    ga.relay(4)
     ga.across(2)
     ga.arrive(1)
-    conv(0, 1, inner, None, {})
+    conv(0, 1, inner, None, {1: doing(ga.relay, 4)})
     ga.arrive(2)
     conv(0, 2, inner, None, {0: doing(ga.turn, 3), 2: doing(ga.relay, 5)})
+    ga.turn(4)
     local_stats(inner, mask, count, ex.mine(1))
     ex.send(1)
-    ga.turn(4)
     ga.across(3)
+    ga.turn(5)
     stats1 = joint_stats(ex, 1)
-    ga.turn(5)
-    put_spare(ex.mine(2), normed(inner_rows, stats1, 1))
+    put_spare(ex.mine(2), normed(inner_rows, stats1, 1, SB))
     ga.arrive(3)
     conv(1, 0, block, lambda it: jnp.concatenate([base_rows(2 * it), base_rows(2 * it + 1)], axis=0),
          {1: doing(ga.across, 4), 3: doing(ga.across, 5)})
     ga.arrive(4)
     for u in range(3):
-        share(u).start()
+        share(u, SB).start()
     conv(1, 1, block, None, {})
     ga.arrive(5)
     conv(1, 2, block, None, {})
@@ -741,22 +746,17 @@
     put_spare(ex.mine(4), low_sums(block, block_rows, stats2, 2, head_rows, sums2))
     turn(block)
     trade.start()
-    first_grad(p, S, dyT, dfl)
+    first_grad(p, SB, dyT, dfl)
     for u in range(3):
-        share(u).wait()
+        share(u, SB).wait()
     trade.wait()
-    filter_grad(p, S, S2, dyT, dyS, DS, mu1, G, 0, dfl)
+    filter_grad(p, SB, S2, dyT, dyS, DS, mu1, G, 0, dfl)
     sc.begin(0)
-    filter_grad(p, S, S2, dyT, dyS, DS, mu1, G, 1, dfl)
+    filter_grad(p, SB, S2, dyT, dyS, DS, mu1, G, 1, dfl)
     sc.begin(1)
-    filter_grad(p, S, S2, dyT, dyS, DS, mu1, G, 2, dfl)
-    sc.mid(0)
-    sc.begin(2)
-    pl.semaphore_signal(free, inc=1, device_id=(p.b, p.sib), device_id_type=MESH)
-
     def spread(src):
         def one(j, carry):
-            spread_rows(S, j, src[rows(j), :])
+            spread_rows(SA, j, src[rows(j), :])
             return carry
 
         lax.fori_loop(0, 8, one, 0)
@@ -765,26 +765,30 @@
 
     def back_conv1(it, carry):
         r0 = pl.multiple_of(it * 384, 384)
-        dfl[pl.ds(r0, 384), :] = conv_back_rows(S, W, 1, r0, 384)
-
-        @pl.when(it == 1)
+        dfl[pl.ds(r0, 384), :] = conv_back_rows(SA, W, 1, r0, 384)
+
+        @pl.when(it == 0)
+        def _():
+            sc.mid(0)
+
+        @pl.when(it == 2)
         def _():
             sc.mid(1)
-
-        @pl.when(it == 3)
-        def _():
-            sc.mid(2)
 
         return carry
 
     lax.fori_loop(0, 4, back_conv1, 0)
     grad_sums(inner_rows, stats1, 1, dfl_rows, 4)
     ex.send(4)
-    normed(base_rows, stats0, 0)
+    sc.along(0)
+    filter_grad(p, SB, S2, dyT, dyS, DS, mu1, G, 2, None)
+    sc.begin(2)
+    pl.semaphore_signal(free, inc=1, device_id=(p.b, p.sib), device_id_type=MESH)
+    normed(base_rows, stats0, 0, SA)
+    sc.along(1)
+    tot4 = ex.total(4)
     pl.semaphore_wait(free, 1)
     share(0).start()
-    sc.along(0)
-    tot4 = ex.total(4)
     sums1 = wide(tot4[0:5]), wide(tot4[8:13])
     lost1 = lost(spare(tot4), mu1)
     put_spare(ex.mine(5), low_sums(dfl, inner_rows, stats1, 1, dfl_rows, sums1))
@@ -792,31 +796,29 @@
     trade.start()
     for u in range(1, 3):
         share(u).start()
-    sc.along(1)
-    first_grad(p, S, dyT, inner)
-    sc.along(2)
+    first_grad(p, SA, dyT, inner)
+    sc.mid(2)
+    squares = sc.final(0, lost1)
     sc.clear(0)
     share(0).wait()
     trade.wait()
-    filter_grad(p, S, S2, dyT, dyS, DS, mu0, G, 3, inner)
+    filter_grad(p, SA, S2, dyT, dyS, DS, mu0, G, 3, inner)
     sc.begin(3)
-    squares = sc.final(0, lost1)
     sc.clear(1)
     share(1).wait()
-    filter_grad(p, S, S2, dyT, dyS, DS, mu0, G, 4, inner)
+    filter_grad(p, SA, S2, dyT, dyS, DS, mu0, G, 4, inner)
     sc.begin(4)
-    squares = squares + sc.final(1, lost1)
+    sc.along(2)
     sc.clear(2)
     share(2).wait()
-    filter_grad(p, S, S2, dyT, dyS, DS, mu0, G, 5, inner)
+    filter_grad(p, SA, S2, dyT, dyS, DS, mu0, G, 5, inner)
     sc.mid(3)
     sc.begin(5)
-    squares = squares + sc.final(2, lost1)
     spread(dfl)
 
     def back_conv0(it, carry):
         r0 = pl.multiple_of(it * 384, 384)
-        inner[pl.ds(r0, 384), :] = conv_back_rows(S, W, 0, r0, 384)
+        inner[pl.ds(r0, 384), :] = conv_back_rows(SA, W, 0, r0, 384)
 
         @pl.when(it == 1)
         def _():
@@ -824,35 +826,46 @@
 
         @pl.when(it == 2)
         def _():
+            sc.clear_line(0)
             sc.along(3)
 
         return carry
 
     lax.fori_loop(0, 4, back_conv0, 0)
 
+    sc.mid(5)
     grad_sums(base_rows, stats0, 0, inner_rows, 5)
     ex.send(5)
-    sc.mid(5)
+    squares = squares + sc.final(1, lost1) + sc.final(2, lost1)
+    sc.clear_line(1)
     sc.along(4)
     tot5 = ex.total(5)
     lost0 = lost(spare(tot5), mu0)
     squares = squares + sc.final(3, lost0)
+    sc.clear_line(2)
+    sc.along(5)
     sums0 = wide(tot5[0:5]), wide(tot5[8:13])
     grid16 = dfl.at[512:640]
     grid16[...] = jnp.zeros((128, C), f32)
     dstem[...] = jnp.zeros((BLK, 128), f32)
 
-    def back0(j, carry):
-        d = block[rows(j), :] + grad_rows(base_rows, stats0, 0, inner_rows, sums0, j)
-        d = d.astype(bf16)
-        pick = iota((BLK, 128), 1) // 16 == j
-        x = jnp.where(pick, stem[...], 0.0).astype(bf16)
-        grid16[...] += lax.dot_general(x, d, CC, preferred_element_type=f32)
-        y = lax.dot_general(d, bridge8, AC, preferred_element_type=f32)
-        dstem[...] += jnp.where(pick, y, 0.0)
+    def back0(i, carry):
+        total_g, total_s = None, None
+        for h in range(4):
+            j = 4 * i + h
+            d = block[rows(j), :] + grad_rows(base_rows, stats0, 0, inner_rows, sums0, j)
+            d = d.astype(bf16)
+            pick = iota((BLK, 128), 1) // 16 == j
+            x = jnp.where(pick, stem[...], 0.0).astype(bf16)
+            g = lax.dot_general(x, d, CC, preferred_element_type=f32)
+            y = jnp.where(pick, lax.dot_general(d, bridge8, AC, preferred_element_type=f32), 0.0)
+            total_g = g if total_g is None else total_g + g
+            total_s = y if total_s is None else total_s + y
+        grid16[...] += total_g
+        dstem[...] += total_s
         return carry
 
-    lax.fori_loop(0, 8, back0, 0)
+    lax.fori_loop(0, 2, back0, 0)
     acc = grid16[0:16, :]
     for j in range(1, 8):
         acc = acc + grid16[16 * j : 16 * j + 16, :]
@@ -864,7 +877,6 @@
 
     give = remote(half(0, 1 - p.c), half(32, 1 - p.c), fs, fr, p.b, p.sib)
     give.start()
-    sc.along(5)
     low = dstem[...].astype(bf16)
     high = lax.Precision.HIGHEST
     acc = None
@@ -924,6 +936,7 @@
         sc.end(e)
     for e in range(3, 6):
         sc.clear(e)
+        sc.clear_line(e)
     for e in range(8):
         ex.drain(e)
 
@@ -943,7 +956,7 @@
         ],
         out_specs=(spec(V),) * 4,
         scratch_shapes=[
-            V((2, 3, NZ, 2, 256, C), bf16), V((3, 10 * BLK, C), bf16), V((3, 10 * BLK, C), bf16),
+            V((2, 3, NZ, 2, 256, C), bf16), V((3, 10 * BLK, C), bf16), V((3, 10 * BLK, C), bf16), V((10 * BLK, C), bf16),
             V((NZ, 2, 80, ROWS), bf16), V((NZ, 80, ROWS), bf16), V((NZ * 80, 128), f32),
             V((ROWS, C), f32), V((ROWS, C), f32), V((ROWS, C), f32),
             V((3, 3, 256, C), bf16), V((6, 3, 64, C), LINE), V((3, NZ, 256, C), bf16), V((3, NZ, 64, C), LINE),
@@ -969,36 +982,63 @@
 
 
 def adam_kernel(G, misc, own, stem_g, *refs):
-    ins, outs = refs[:18], refs[18:]
+    ins, outs, (norm_o, loss_o, held, lsem, osem) = refs[:18], refs[18:36], refs[36:]
+    norm_o[...] = misc[0:1, 0:1]
+    loss_o[...] = misc[1:2, 0:1]
     factor = clip_norm / jnp.maximum(misc[0:1, :], clip_norm)
+    wide_factor = jnp.concatenate([factor] * 5, axis=1)
+
+    def load(s, i):
+        return pltpu.make_async_copy(ins[i].at[s // 3, s % 3], held.at[i, s], lsem.at[i, s])
+
+    def store(s, i):
+        return pltpu.make_async_copy(held.at[i, s], outs[i].at[s // 3, s % 3], osem.at[i, s])
+
+    for s in range(6):
+        for i in range(3):
+            load(s, i).start()
 
     def write(i, g, rate, shrink, f):
         w, m, v = (r[...] for r in ins[3 * i : 3 * i + 3])
         for o, x in zip(outs[3 * i : 3 * i + 3], adam_rule(g, w, m, v, rate, shrink, f)):
             o[...] = x
 
-    g = G[0, 0, 0:240, :].astype(f32)
-    write(0, g[None, None], 0.033, 0.05, jnp.concatenate([factor] * 5, axis=1)[None, None])
-
-    @pl.when((pl.program_id(0) == 0) & (pl.program_id(1) == 0))
-    def _():
-        write(1, stem_g[:, 0:27], 0.5, 0.05, factor[:, 0:27])
-        write(2, own[0:16, 0:80], 0.6, 0.05, factor[:, 0:80])
-        write(3, own[32:38, 0:80], 0.5, 0.0, factor[:, 0:80])
-        write(4, own[16:26, 0:80], 0.1, 0.05, factor[:, 0:80])
-        write(5, misc[2:3, 0:10], 0.5, 0.0, factor[:, 0:10])
+    write(1, stem_g[:, 0:27], 0.5, 0.05, factor[:, 0:27])
+    write(2, own[0:16, 0:80], 0.6, 0.05, factor[:, 0:80])
+    write(3, own[32:38, 0:80], 0.5, 0.0, factor[:, 0:80])
+    write(4, own[16:26, 0:80], 0.1, 0.05, factor[:, 0:80])
+    write(5, misc[2:3, 0:10], 0.5, 0.0, factor[:, 0:10])
+    for s in range(6):
+        for i in range(3):
+            load(s, i).wait()
+
+        def part(j, carry):
+            at = pl.ds(pl.multiple_of(j * 48, 16), 48)
+            new = adam_rule(
+                G[s // 3, s % 3, at, :].astype(f32), held[0, s, at, :], held[1, s, at, :], held[2, s, at, :],
+                0.033, 0.05, wide_factor,
+            )
+            for i in range(3):
+                held[i, s, at, :] = new[i]
+            return carry
+
+        lax.fori_loop(0, 5, part, 0)
+        for i in range(3):
+            store(s, i).start()
+    for s in range(6):
+        for i in range(3):
+            store(s, i).wait()
 
 
 def adam_call(G, misc, own, stem_g, *state):
-    whole = lambda x: pl.BlockSpec(x.shape, lambda k, u: (0,) * x.ndim)
-    tile = lambda n: pl.BlockSpec((1, 1, n, C), lambda k, u: (k, u, 0, 0))
-    specs = [tile(240)] * 3 + [whole(x) for x in state[3:]]
+    V, A, D = pltpu.VMEM, pl.ANY, pltpu.SemaphoreType.DMA
+    spec = lambda m: pl.BlockSpec(memory_space=m)
     return pl.pallas_call(
         adam_kernel,
-        out_shape=tuple(jax.ShapeDtypeStruct(x.shape, f32) for x in state),
-        grid=(2, 3),
-        in_specs=[tile(256), whole(misc), whole(own), whole(stem_g)] + specs,
-        out_specs=tuple(specs),
+        out_shape=tuple(jax.ShapeDtypeStruct(s, f32) for s in [x.shape for x in state] + [(1, 1)] * 2),
+        in_specs=[spec(V)] * 4 + [spec(A)] * 3 + [spec(V)] * 15,
+        out_specs=tuple([spec(A)] * 3 + [spec(V)] * 17),
+        scratch_shapes=[V((3, 6, 240, C), f32), D((3, 6)), D((3, 6))],
         compiler_params=pltpu.CompilerParams(vmem_limit_bytes=62 << 20),
     )(G, misc, own, stem_g, *state)
 
@@ -1343,8 +1383,8 @@
         *norm,
         *head,
         *(x[0] for x in bias),
-        misc[0, 0],
-        misc[1, 0],
+        new[18].reshape(()),
+        new[19].reshape(()),
     )
 
 

time: 259 us -> 245 us (0.946)
  Pallas kernels: 257 us -> 244 us
    pallas_call x1, Pallas kernels: 245 us -> 233 us  [step_call(): pl.pallas_call(step_kernel, out_shape=(sh((2, 3, 256, C), bf16), sh((40,...]
where the time goes in v3:
time: 245 us
  Pallas kernels  244 us (100%)
    pallas_call x1, Pallas kernels, step_call(): pl.pallas_call(step_kernel, out_shape=(sh((2, 3, 256, C), bf16), sh((40,...  233 us
    pallas_call x1, Pallas kernels, adam_call(): pl.pallas_call(adam_kernel, out_shape=tuple((jax.ShapeDtypeStruct(s, f32)...  11.3 us

profile of v3, /device:TPU:1, one launch (start us, length us, event | category | flops | bytes accessed | tf_op | source)
XLA Modules:
  0.0 244.7 jit_solution(197535191021424715)
XLA Ops:
  0.7 232.6 %shard_map.374 = (bf16[2,3,256,640]{3,2,1,0:T(8,128)(2,1)}, f32[40,128]{1,0:T(8,128)}, f32[16,128]{1,0:T(8,128)}, f32[8,128]{1,0:T(8,128)}) custom-call(bf16[24,3072]{1,0:T(8,128)(2,1)} %images.1, s32[1,24]{1,0:T(1,128)} %bitcast.47, s32[1,24]{1,0:T(1,128)} %bitcast.48, s32[1,24]{1,0:T(1,128)} %bitcast.49, s32[4,8]{1,0:T(4,128)} %sizes.1, f32[16,27]{1,0:T(8,128)} %refs_3_.1, ...), custom_call_target="tpu_custom_call" | custom-call | tf_op jit(solution)/shard_map/pallas_call | solution.py:949
  233.2 11.3 %shard_map.375 = (f32[2,3,240,640]{3,2,1,0:T(8,128)}, f32[2,3,240,640]{3,2,1,0:T(8,128)}, f32[2,3,240,640]{3,2,1,0:T(8,128)}, f32[16,27]{1,0:T(8,128)}, f32[16,2...) custom-call(bf16[2,3,256,640]{3,2,1,0:T(8,128)(2,1)} %get-tuple-elem, ...), custom_call_target="tpu_custom_call" | custom-call | tf_op jit(solution)/shard_map/pallas_call | solution.py:1036

commit v4 on v3

--- a/solution.py
+++ b/solution.py
@@ -352,6 +352,61 @@
             self.out4(e, d).wait()
 
 
+class RowSum:
+    def __init__(self, p, ref, ssem, rsem):
+        self.p, self.ref, self.ssem, self.rsem = p, ref, ssem, rsem
+
+    def eight(self, t, row, i):
+        return self.ref.at[t, pl.ds(pl.multiple_of(row + 8 * i, 8), 8), :]
+
+    def hop(self, t, n, src, dst, b, f):
+        return remote(src, dst, self.ssem.at[t, n], self.rsem.at[t, n], b, f)
+
+    def three(self, t, n, row):
+        rest = self.ref.at[t, row : row + 24, :]
+        return self.hop(t, n, rest, rest, self.p.b, self.p.sib)
+
+    def give(self, t):
+        p = self.p
+        return self.hop(t, 0, self.eight(t, 0, 1 - p.c), self.eight(t, 16, 1 - p.c), p.b, p.sib)
+
+    def along(self, t):
+        p = self.p
+        self.give(t).wait_recv()
+        mine = self.eight(t, 32, p.z)
+        mine[...] = self.eight(t, 0, p.c)[...] + self.eight(t, 16, p.c)[...]
+        for i in (2, 1, 3):
+            self.hop(t, 1, mine, mine, p.b, 2 * lax.rem(p.z + i, NZ) + p.c).start()
+
+    def square(self, t):
+        p = self.p
+        self.three(t, 1, 32).wait_recv()
+        mine = self.eight(t, 64, p.b)
+        mine[...] = jnp.sum(self.ref[t, 32:64, :].reshape(NZ, 8, C), axis=0)
+        for to in (p.dn, p.xn, p.yn):
+            self.hop(t, 2, mine, mine, to, p.f).start()
+
+    def back(self, t):
+        p = self.p
+        mine = self.eight(t, 96, p.c)
+        return self.hop(t, 3, mine, mine, p.b, p.sib)
+
+    def close(self, t):
+        self.three(t, 2, 64).wait_recv()
+        self.eight(t, 96, self.p.c)[...] = jnp.sum(self.ref[t, 64:96, :].reshape(NB, 8, C), axis=0)
+        self.back(t).start()
+
+    def result(self, t):
+        self.back(t).wait_recv()
+        return self.ref[t, 96:112, :]
+
+    def drain(self, t):
+        self.give(t).wait_send()
+        self.three(t, 1, 32).wait_send()
+        self.three(t, 2, 64).wait_send()
+        self.back(t).wait_send()
+
+
 def conv_back_rows(S, W, k, r0, M):
     acc = None
     for u in range(3):
@@ -415,14 +470,15 @@
 def step_kernel(
     images, labels, partner, valid, sizes, stem_w, bridge_t, conv_w, norm, head, bias,
     GF, own_o, stem_o, misc_o,
-    W, S, S2, S3, dyT, dyS, DS, inner, block, dfl, RX, RZ, G, Q, slots, sibs, lab, gath, par, mask, AB, stem, dstem, pad,
+    W, S, S2, S3, dyT, dyS, DS, inner, block, dfl, RX, RZ, G, Q, slots, sibs, lab, few, gath, par, mask, AB, stem, dstem, pad,
     xs_, xr_, ps_, pr_, lbs, lbr, gs, gr, zs, zr, xs, xr, ds, dr, ls,
-    bs, br, cs, cr, es, er, ts, tr, us, ur, free, fs, fr, hs, hr, js, jr, ms, mr,
+    bs, br, cs, cr, es, er, ts, tr, us, ur, free, fs, fr,
 ):
     p = Place()
     ex = Exchange(p, slots, sibs, xs_, xr_, ps_, pr_)
     ga = Gather(p, W, zs, zr, xs, xr, ds, dr)
     sc = Scatter(p, W, RX, RZ, G, Q, GF, (bs, br, cs, cr, es, er))
+    rs = RowSum(p, few, fs, fr)
     greet(p)
     SA = [S.at[u] for u in range(3)]
     SB = [S.at[0], S.at[1], S3]
@@ -454,7 +510,7 @@
     ga.zsend(0)
     for s in range(1, 6):
         cast(s)
-        if s < 3:
+        if s < 2:
             ga.zsend(s)
     img = pltpu.roll(images[...].astype(f32), 32, 1)
     lane = iota((IMG, 128), 1)
@@ -547,9 +603,10 @@
     lax.fori_loop(0, 8, base_block, 0)
     local_stats(inner, mask, count, ex.mine(0))
     ex.send(0)
+    ga.zsend(2)
     ga.relay(0)
+    ga.turn(0)
     ga.relay(1)
-    ga.turn(0)
 
     def inner_rows(j):
         return inner[rows(j), :]
@@ -679,7 +736,8 @@
     )
     d_logits = jnp.where(live, (jnp.exp(logp) - target) * (weight / total), 0.0).astype(bf16)
     g_bias = jnp.sum(d_logits.astype(f32), axis=0, keepdims=True)
-    par[24:40, :] = lax.dot_general(d_logits, pooled, CC, preferred_element_type=f32)
+    few[0, 0:16, :] = lax.dot_general(d_logits, pooled, CC, preferred_element_type=f32)
+    rs.give(0).start()
     d_pooled = jnp.dot(d_logits, head16, preferred_element_type=f32)
     d_out24 = d_pooled / 64.0
 
@@ -754,6 +812,7 @@
     sc.begin(0)
     filter_grad(p, SB, S2, dyT, dyS, DS, mu1, G, 1, dfl)
     sc.begin(1)
+    rs.along(0)
     def spread(src):
         def one(j, carry):
             spread_rows(SA, j, src[rows(j), :])
@@ -783,6 +842,7 @@
     sc.along(0)
     filter_grad(p, SB, S2, dyT, dyS, DS, mu1, G, 2, None)
     sc.begin(2)
+    rs.square(0)
     pl.semaphore_signal(free, inc=1, device_id=(p.b, p.sib), device_id_type=MESH)
     normed(base_rows, stats0, 0, SA)
     sc.along(1)
@@ -804,6 +864,7 @@
     trade.wait()
     filter_grad(p, SA, S2, dyT, dyS, DS, mu0, G, 3, inner)
     sc.begin(3)
+    rs.close(0)
     sc.clear(1)
     share(1).wait()
     filter_grad(p, SA, S2, dyT, dyS, DS, mu0, G, 4, inner)
@@ -869,14 +930,8 @@
     acc = grid16[0:16, :]
     for j in range(1, 8):
         acc = acc + grid16[16 * j : 16 * j + 16, :]
-    dfl[0:16, :] = acc
-    dfl[16:32, :] = par[24:40, :]
-
-    def half(row, c):
-        return dfl.at[pl.ds(pl.multiple_of(row + 16 * c, 16), 16), :]
-
-    give = remote(half(0, 1 - p.c), half(32, 1 - p.c), fs, fr, p.b, p.sib)
-    give.start()
+    few[1, 0:16, :] = acc
+    rs.give(1).start()
     low = dstem[...].astype(bf16)
     high = lax.Precision.HIGHEST
     acc = None
@@ -893,32 +948,15 @@
         tile_c.astype(f32), acc, precision=high, preferred_element_type=f32
     )
     ex.send(6)
-    give.wait()
-    zline = dfl.at[pl.ds(pl.multiple_of(64 + 16 * p.z, 16), 16), :]
-    zline[...] = half(0, p.c)[...] + half(32, p.c)[...]
-    for i in range(1, NZ):
-        to = lax.rem(p.z + i, NZ)
-        remote(zline, zline, hs, hr, p.b, 2 * to + p.c).start()
+    rs.along(1)
     squares = squares + sc.final(4, lost0)
-    rest = dfl.at[64 : 64 + 16 * (NZ - 1), :]
-    remote(rest, rest, hs, hr, p.b, p.sib).wait()
-    square = dfl.at[pl.ds(pl.multiple_of(128 + 16 * p.b, 16), 16), :]
-    square[...] = jnp.sum(dfl[64:128, :].reshape(NZ, 16, C), axis=0)
-    for i in range(1, NB):
-        to = lax.rem(p.b + i, NB)
-        remote(square, square, js, jr, to, p.f).start()
+    rs.square(1)
     g_stem = ex.total(6)
     squares = squares + sc.final(5, lost0)
     slots[7, p.chip] = jnp.full((16, 128), jnp.sum(squares), f32)
     ex.send(7)
-    rest = dfl.at[128 : 128 + 16 * (NB - 1), :]
-    remote(rest, rest, js, jr, p.b, p.sib).wait()
-    done = half(192, p.c)
-    done[...] = jnp.sum(dfl[128:192, :].reshape(NB, 16, C), axis=0)
-    give = remote(done, done, ms, mr, p.b, p.sib)
-    give.start()
-    give.wait()
-    both = dfl[192:224, :]
+    rs.close(1)
+    both = jnp.concatenate([rs.result(1), rs.result(0)], axis=0)
     bias_all = tot3[6:7, :]
     stem_o[...] = g_stem
     ng = [row for sums in (sums0, sums1, sums2) for row in (sums[1], sums[0])]
@@ -939,6 +977,8 @@
         sc.clear_line(e)
     for e in range(8):
         ex.drain(e)
+    rs.drain(0)
+    rs.drain(1)
 
 
 def step_call(images, labels, partner, valid, sizes, stem_w, bridge_t, conv_w, norm, head, bias):
@@ -960,11 +1000,11 @@
             V((NZ, 2, 80, ROWS), bf16), V((NZ, 80, ROWS), bf16), V((NZ * 80, 128), f32),
             V((ROWS, C), f32), V((ROWS, C), f32), V((ROWS, C), f32),
             V((3, 3, 256, C), bf16), V((6, 3, 64, C), LINE), V((3, NZ, 256, C), bf16), V((3, NZ, 64, C), LINE),
-            V((8, NCHIP, 16, 128), f32), V((8, 2, 16, 128), f32), V((2, NCHIP, 128), f32), V((NZ, 2, 40, 128), f32), V((40, C), f32),
+            V((8, NCHIP, 16, 128), f32), V((8, 2, 16, 128), f32), V((2, NCHIP, 128), f32), V((2, 112, C), f32), V((NZ, 2, 40, 128), f32), V((40, C), f32),
             V((BLK, 128), f32), V((BLK, 384), f32), V((BLK, 128), f32), V((BLK, 128), f32), V((8, 128), f32),
             D((8,)), D((8,)), D((8,)), D((8,)), D, D, D((2,)), D((2,)), D((6, 4)), D((6, 4)), D((6, 12)), D((6, 12)), D((6,)), D((6,)), D((6,)),
             D((6, 6)), D((6, 6)), D((6, 3)), D((6, 3)), D((6, 3)), D((6, 3)), D((3,)), D((3,)), D, D,
-            pltpu.SemaphoreType.REGULAR, D, D, D, D, D, D, D, D,
+            pltpu.SemaphoreType.REGULAR, D((2, 4)), D((2, 4)),
         ],
         compiler_params=pltpu.CompilerParams(
             collective_id=0, has_side_effects=True, vmem_limit_bytes=63 << 20
@@ -982,7 +1022,7 @@
 
 
 def adam_kernel(G, misc, own, stem_g, *refs):
-    ins, outs, (norm_o, loss_o, held, lsem, osem) = refs[:18], refs[18:36], refs[36:]
+    ins, outs, (norm_o, loss_o, held, GV, lsem, osem, gsem) = refs[:18], refs[18:36], refs[36:]
     norm_o[...] = misc[0:1, 0:1]
     loss_o[...] = misc[1:2, 0:1]
     factor = clip_norm / jnp.maximum(misc[0:1, :], clip_norm)
@@ -994,7 +1034,11 @@
     def store(s, i):
         return pltpu.make_async_copy(held.at[i, s], outs[i].at[s // 3, s % 3], osem.at[i, s])
 
+    def grad(s):
+        return pltpu.make_async_copy(G.at[s // 3, s % 3], GV.at[s], gsem.at[s])
+
     for s in range(6):
+        grad(s).start()
         for i in range(3):
             load(s, i).start()
 
@@ -1011,11 +1055,12 @@
     for s in range(6):
         for i in range(3):
             load(s, i).wait()
+        grad(s).wait()
 
         def part(j, carry):
             at = pl.ds(pl.multiple_of(j * 48, 16), 48)
             new = adam_rule(
-                G[s // 3, s % 3, at, :].astype(f32), held[0, s, at, :], held[1, s, at, :], held[2, s, at, :],
+                GV[s, at, :].astype(f32), held[0, s, at, :], held[1, s, at, :], held[2, s, at, :],
                 0.033, 0.05, wide_factor,
             )
             for i in range(3):
@@ -1036,9 +1081,9 @@
     return pl.pallas_call(
         adam_kernel,
         out_shape=tuple(jax.ShapeDtypeStruct(s, f32) for s in [x.shape for x in state] + [(1, 1)] * 2),
-        in_specs=[spec(V)] * 4 + [spec(A)] * 3 + [spec(V)] * 15,
+        in_specs=[spec(A)] + [spec(V)] * 3 + [spec(A)] * 3 + [spec(V)] * 15,
         out_specs=tuple([spec(A)] * 3 + [spec(V)] * 17),
-        scratch_shapes=[V((3, 6, 240, C), f32), D((3, 6)), D((3, 6))],
+        scratch_shapes=[V((3, 6, 240, C), f32), V((6, 256, C), bf16), D((3, 6)), D((3, 6)), D((6,))],
         compiler_params=pltpu.CompilerParams(vmem_limit_bytes=62 << 20),
     )(G, misc, own, stem_g, *state)
 

time: 245 us -> 239 us (0.976)
  Pallas kernels: 244 us -> 238 us
    pallas_call x1, Pallas kernels: 233 us -> 228 us  [step_call(): pl.pallas_call(step_kernel, out_shape=(sh((2, 3, 256, C), bf16), sh((40,...]
where the time goes in v4:
time: 239 us
  Pallas kernels  238 us (100%)
    pallas_call x1, Pallas kernels, step_call(): pl.pallas_call(step_kernel, out_shape=(sh((2, 3, 256, C), bf16), sh((40,...  228 us
    pallas_call x1, Pallas kernels, adam_call(): pl.pallas_call(adam_kernel, out_shape=tuple((jax.ShapeDtypeStruct(s, f32)...  10 us

profile of v4, /device:TPU:1, one launch (start us, length us, event | category | flops | bytes accessed | tf_op | source)
XLA Modules:
  0.0 239.0 jit_solution(16989174884466533351)
XLA Ops:
  0.7 228.1 %shard_map.374 = (bf16[2,3,256,640]{3,2,1,0:T(8,128)(2,1)}, f32[40,128]{1,0:T(8,128)}, f32[16,128]{1,0:T(8,128)}, f32[8,128]{1,0:T(8,128)}) custom-call(bf16[24,3072]{1,0:T(8,128)(2,1)} %images.1, s32[1,24]{1,0:T(1,128)} %bitcast.47, s32[1,24]{1,0:T(1,128)} %bitcast.48, s32[1,24]{1,0:T(1,128)} %bitcast.49, s32[4,8]{1,0:T(4,128)} %sizes.1, f32[16,27]{1,0:T(8,128)} %refs_3_.1, ...), custom_call_target="tpu_custom_call" | custom-call | tf_op jit(solution)/shard_map/pallas_call | solution.py:989
  228.8 10.0 %shard_map.375 = (f32[2,3,240,640]{3,2,1,0:T(8,128)}, f32[2,3,240,640]{3,2,1,0:T(8,128)}, f32[2,3,240,640]{3,2,1,0:T(8,128)}, f32[16,27]{1,0:T(8,128)}, f32[16,2...) custom-call(bf16[2,3,256,640]{3,2,1,0:T(8,128)(2,1)} %get-tuple-elem, ...), custom_call_target="tpu_custom_call" | custom-call | tf_op jit(solution)/shard_map/pallas_call | solution.py:1081

commit v5 on v4

--- a/solution.py
+++ b/solution.py
@@ -81,18 +81,21 @@
         self.p, self.slots, self.sibs = p, slots, sibs
         self.ssem, self.rsem, self.psem, self.qsem = ssem, rsem, psem, qsem
 
+    def rows(self, e):
+        return 8 if e == 7 else 16
+
     def mine(self, e):
         return self.slots.at[e, self.p.chip]
 
     def send(self, e):
         p = self.p
-        mine = self.mine(e)
+        mine = self.mine(e).at[0 : self.rows(e)]
         for b, z in peers(p):
             remote(mine, mine, self.ssem.at[e], self.rsem.at[e], b, 2 * z + p.c).start()
 
     def rest(self, e):
         p = self.p
-        rest = self.slots.at[e, 0 : NCHIP - 1]
+        rest = self.slots.at[e, 0 : NCHIP - 1, 0 : self.rows(e)]
         return remote(rest, rest, self.ssem.at[e], self.rsem.at[e], p.b, p.sib)
 
     def across(self, e):
@@ -373,18 +376,18 @@
     def along(self, t):
         p = self.p
         self.give(t).wait_recv()
-        mine = self.eight(t, 32, p.z)
+        mine = self.eight(t, 32, p.b)
         mine[...] = self.eight(t, 0, p.c)[...] + self.eight(t, 16, p.c)[...]
-        for i in (2, 1, 3):
-            self.hop(t, 1, mine, mine, p.b, 2 * lax.rem(p.z + i, NZ) + p.c).start()
+        for to in (p.dn, p.xn, p.yn):
+            self.hop(t, 1, mine, mine, to, p.f).start()
 
     def square(self, t):
         p = self.p
         self.three(t, 1, 32).wait_recv()
-        mine = self.eight(t, 64, p.b)
-        mine[...] = jnp.sum(self.ref[t, 32:64, :].reshape(NZ, 8, C), axis=0)
-        for to in (p.dn, p.xn, p.yn):
-            self.hop(t, 2, mine, mine, to, p.f).start()
+        mine = self.eight(t, 64, p.z)
+        mine[...] = jnp.sum(self.ref[t, 32:64, :].reshape(NB, 8, C), axis=0)
+        for i in (2, 1, 3):
+            self.hop(t, 2, mine, mine, p.b, 2 * lax.rem(p.z + i, NZ) + p.c).start()
 
     def back(self, t):
         p = self.p
@@ -393,7 +396,7 @@
 
     def close(self, t):
         self.three(t, 2, 64).wait_recv()
-        self.eight(t, 96, self.p.c)[...] = jnp.sum(self.ref[t, 64:96, :].reshape(NB, 8, C), axis=0)
+        self.eight(t, 96, self.p.c)[...] = jnp.sum(self.ref[t, 64:96, :].reshape(NZ, 8, C), axis=0)
         self.back(t).start()
 
     def result(self, t):
@@ -469,10 +472,10 @@
 
 def step_kernel(
     images, labels, partner, valid, sizes, stem_w, bridge_t, conv_w, norm, head, bias,
-    GF, own_o, stem_o, misc_o,
-    W, S, S2, S3, dyT, dyS, DS, inner, block, dfl, RX, RZ, G, Q, slots, sibs, lab, few, gath, par, mask, AB, stem, dstem, pad,
+    GF_o, own_o, stem_o, misc_o,
+    GF, W, S, S2, S3, dyT, dyS, DS, inner, block, dfl, RX, RZ, G, Q, slots, sibs, lab, few, gath, gathn, par, mask, AB, stem, dstem, pad, pad32,
     xs_, xr_, ps_, pr_, lbs, lbr, gs, gr, zs, zr, xs, xr, ds, dr, ls,
-    bs, br, cs, cr, es, er, ts, tr, us, ur, free, fs, fr,
+    bs, br, cs, cr, es, er, ts, tr, us, ur, free, fs, fr, os_,
 ):
     p = Place()
     ex = Exchange(p, slots, sibs, xs_, xr_, ps_, pr_)
@@ -488,11 +491,12 @@
 
     for s in range(6):
         load(s).start()
-    mine = gath.at[p.z, p.c]
-    mine[...] = jnp.zeros((40, 128), f32)
-    mine[0:16, 0:80] = bridge_t[...]
-    mine[16:22, 0:80] = norm[...]
-    mine[24:34, 0:80] = head[...]
+    pad32[...] = jnp.zeros((32, 128), f32)
+    pad32[0:16, 0:80] = bridge_t[...]
+    pad32[16:26, 0:80] = head[...]
+    gath[p.z, p.c] = pad32[...].astype(bf16)
+    gathn[p.z, p.c] = jnp.zeros((8, 128), f32)
+    gathn[p.z, p.c, 0:6, 0:80] = norm[...]
 
     def cast(s):
         load(s).wait()
@@ -506,7 +510,9 @@
     met()
     for i in (2, 1, 3):
         to = lax.rem(p.z + i, NZ)
-        remote(mine, mine, gs.at[0], gr.at[0], p.b, 2 * to + p.c).start()
+        for n, ref in enumerate((gath, gathn)):
+            mine = ref.at[p.z, p.c]
+            remote(mine, mine, gs.at[n], gr.at[n], p.b, 2 * to + p.c).start()
     ga.zsend(0)
     for s in range(1, 6):
         cast(s)
@@ -571,19 +577,24 @@
         S[u, 9 * BLK : 10 * BLK, :] = edge
         for z in range(NZ):
             G[u, z, 240:256, :] = jnp.zeros((16, C), bf16)
-    rest = gath.at[0 : NZ - 1, 0]
-    remote(rest, rest, gs.at[0], gr.at[0], p.b, p.sib).wait()
-    side = gath.at[:, p.c]
-    pair = remote(side, side, gs.at[1], gr.at[1], p.b, p.sib)
-    pair.start()
-    pair.wait()
+    pairs = []
+    for n, ref in enumerate((gath, gathn)):
+        rest = ref.at[0 : NZ - 1, 0]
+        remote(rest, rest, gs.at[n], gr.at[n], p.b, p.sib).wait()
+        side = ref.at[:, p.c]
+        pairs.append(remote(side, side, gs.at[2 + n], gr.at[2 + n], p.b, p.sib))
+        pairs[n].start()
+    for pair in pairs:
+        pair.wait()
     lane = iota((40, 128), 1)
     for k in range(5):
         acc = jnp.zeros((40, 128), f32)
         for f in range(NF):
             lo, hi = max(80 * f, 128 * k), min(80 * f + 80, 128 * k + 128)
             if lo < hi:
-                turned = pltpu.roll(gath[f // 2, f % 2], (80 * f - 128 * k) % 128, 1)
+                low = gath[f // 2, f % 2].astype(f32)
+                all_rows = jnp.concatenate([low[0:16], gathn[f // 2, f % 2], low[16:32]], axis=0)
+                turned = pltpu.roll(all_rows, (80 * f - 128 * k) % 128, 1)
                 acc = jnp.where((lane >= lo - 128 * k) & (lane < hi - 128 * k), turned, acc)
         par[:, 128 * k : 128 * k + 128] = acc
     bridge8 = jnp.concatenate([par[0:16, :].astype(bf16)] * 8, axis=0)
@@ -955,6 +966,14 @@
     squares = squares + sc.final(5, lost0)
     slots[7, p.chip] = jnp.full((16, 128), jnp.sum(squares), f32)
     ex.send(7)
+
+    def leave(e):
+        at = 1 - e // 3, e % 3
+        return pltpu.make_async_copy(GF.at[at], GF_o.at[at], os_.at[e])
+
+    for e in range(4):
+        sc.end(e)
+        leave(e).start()
     rs.close(1)
     both = jnp.concatenate([rs.result(1), rs.result(0)], axis=0)
     bias_all = tot3[6:7, :]
@@ -970,8 +989,9 @@
     misc_o[0:1, :] = jnp.sqrt(conv_sq + other)
     misc_o[1:2, :] = tot3[5:6, :] / total
     misc_o[2:3, :] = bias_all
-    for e in range(6):
+    for e in range(4, 6):
         sc.end(e)
+        leave(e).start()
     for e in range(3, 6):
         sc.clear(e)
         sc.clear_line(e)
@@ -979,6 +999,8 @@
         ex.drain(e)
     rs.drain(0)
     rs.drain(1)
+    for e in range(6):
+        leave(e).wait()
 
 
 def step_call(images, labels, partner, valid, sizes, stem_w, bridge_t, conv_w, norm, head, bias):
@@ -994,17 +1016,17 @@
         in_specs=[
             spec(V), spec(V), spec(V), spec(V), spec(SM), spec(V), spec(V), spec(A), spec(V), spec(V), spec(V),
         ],
-        out_specs=(spec(V),) * 4,
+        out_specs=(spec(A),) + (spec(V),) * 3,
         scratch_shapes=[
-            V((2, 3, NZ, 2, 256, C), bf16), V((3, 10 * BLK, C), bf16), V((3, 10 * BLK, C), bf16), V((10 * BLK, C), bf16),
+            V((2, 3, 256, C), bf16), V((2, 3, NZ, 2, 256, C), bf16), V((3, 10 * BLK, C), bf16), V((3, 10 * BLK, C), bf16), V((10 * BLK, C), bf16),
             V((NZ, 2, 80, ROWS), bf16), V((NZ, 80, ROWS), bf16), V((NZ * 80, 128), f32),
             V((ROWS, C), f32), V((ROWS, C), f32), V((ROWS, C), f32),
             V((3, 3, 256, C), bf16), V((6, 3, 64, C), LINE), V((3, NZ, 256, C), bf16), V((3, NZ, 64, C), LINE),
-            V((8, NCHIP, 16, 128), f32), V((8, 2, 16, 128), f32), V((2, NCHIP, 128), f32), V((2, 112, C), f32), V((NZ, 2, 40, 128), f32), V((40, C), f32),
-            V((BLK, 128), f32), V((BLK, 384), f32), V((BLK, 128), f32), V((BLK, 128), f32), V((8, 128), f32),
-            D((8,)), D((8,)), D((8,)), D((8,)), D, D, D((2,)), D((2,)), D((6, 4)), D((6, 4)), D((6, 12)), D((6, 12)), D((6,)), D((6,)), D((6,)),
+            V((8, NCHIP, 16, 128), f32), V((8, 2, 16, 128), f32), V((2, NCHIP, 128), f32), V((2, 112, C), f32), V((NZ, 2, 32, 128), bf16), V((NZ, 2, 8, 128), f32), V((40, C), f32),
+            V((BLK, 128), f32), V((BLK, 384), f32), V((BLK, 128), f32), V((BLK, 128), f32), V((8, 128), f32), V((32, 128), f32),
+            D((8,)), D((8,)), D((8,)), D((8,)), D, D, D((4,)), D((4,)), D((6, 4)), D((6, 4)), D((6, 12)), D((6, 12)), D((6,)), D((6,)), D((6,)),
             D((6, 6)), D((6, 6)), D((6, 3)), D((6, 3)), D((6, 3)), D((6, 3)), D((3,)), D((3,)), D, D,
-            pltpu.SemaphoreType.REGULAR, D((2, 4)), D((2, 4)),
+            pltpu.SemaphoreType.REGULAR, D((2, 4)), D((2, 4)), D((6,)),
         ],
         compiler_params=pltpu.CompilerParams(
             collective_id=0, has_side_effects=True, vmem_limit_bytes=63 << 20

time: 239 us -> 237 us (level)
  Pallas kernels: 238 us -> 235 us
    pallas_call x1, Pallas kernels: 228 us -> 225 us  [step_call(): pl.pallas_call(step_kernel, out_shape=(sh((2, 3, 256, C), bf16), sh((40,...]
where the time goes in v5:
time: 237 us; the launch traced here: 236 us
  Pallas kernels  235 us (99%)
    pallas_call x1, Pallas kernels, step_call(): pl.pallas_call(step_kernel, out_shape=(sh((2, 3, 256, C), bf16), sh((40,...  225 us
    pallas_call x1, Pallas kernels, adam_call(): pl.pallas_call(adam_kernel, out_shape=tuple((jax.ShapeDtypeStruct(s, f32)...  10 us

profile of v5, /device:TPU:1, one launch (start us, length us, event | category | flops | bytes accessed | tf_op | source)
XLA Modules:
  0.0 236.3 jit_solution(4158273776959924636)
XLA Ops:
  0.7 225.4 %shard_map.374 = (bf16[2,3,256,640]{3,2,1,0:T(8,128)(2,1)}, f32[40,128]{1,0:T(8,128)}, f32[16,128]{1,0:T(8,128)}, f32[8,128]{1,0:T(8,128)}) custom-call(bf16[24,3072]{1,0:T(8,128)(2,1)} %images.1, s32[1,24]{1,0:T(1,128)} %bitcast.47, s32[1,24]{1,0:T(1,128)} %bitcast.48, s32[1,24]{1,0:T(1,128)} %bitcast.49, s32[4,8]{1,0:T(4,128)} %sizes.1, f32[16,27]{1,0:T(8,128)} %refs_3_.1, ...), custom_call_target="tpu_custom_call" | custom-call | tf_op jit(solution)/shard_map/pallas_call | solution.py:1011
  226.0 10.0 %shard_map.375 = (f32[2,3,240,640]{3,2,1,0:T(8,128)}, f32[2,3,240,640]{3,2,1,0:T(8,128)}, f32[2,3,240,640]{3,2,1,0:T(8,128)}, f32[16,27]{1,0:T(8,128)}, f32[16,2...) custom-call(bf16[2,3,256,640]{3,2,1,0:T(8,128)(2,1)} %get-tuple-elem, ...), custom_call_target="tpu_custom_call" | custom-call | tf_op jit(solution)/shard_map/pallas_call | solution.py:1103

commit v6 on v5

--- a/solution.py
+++ b/solution.py
@@ -677,7 +677,7 @@
     ga.turn(1)
     ga.across(0)
     ga.arrive(0)
-    conv(0, 0, inner, 0, {0: doing(ga.turn, 2), 1: doing(ga.relay, 3)})
+    conv(0, 0, inner, 0, {1: doing(ga.turn, 2), 2: doing(ga.relay, 3)})
     ga.across(1)
     ga.across(2)
     ga.arrive(1)
@@ -913,9 +913,9 @@
     sc.along(4)
     tot5 = ex.total(5)
     lost0 = lost(spare(tot5), mu0)
-    squares = squares + sc.final(3, lost0)
     sc.clear_line(2)
     sc.along(5)
+    squares = squares + sc.final(3, lost0)
     sums0 = wide(tot5[0:5]), wide(tot5[8:13])
     grid16 = dfl.at[512:640]
     grid16[...] = jnp.zeros((128, C), f32)

time: 237 us -> 235 us (level)
  no operation moved by 1% of the time
where the time goes in v6:
time: 235 us
  Pallas kernels  234 us (100%)
    pallas_call x1, Pallas kernels, step_call(): pl.pallas_call(step_kernel, out_shape=(sh((2, 3, 256, C), bf16), sh((40,...  224 us
    pallas_call x1, Pallas kernels, adam_call(): pl.pallas_call(adam_kernel, out_shape=tuple((jax.ShapeDtypeStruct(s, f32)...  10 us

profile of v6, /device:TPU:1, one launch (start us, length us, event | category | flops | bytes accessed | tf_op | source)
XLA Modules:
  0.0 235.2 jit_solution(464323247535478309)
XLA Ops:
  0.7 224.3 %shard_map.374 = (bf16[2,3,256,640]{3,2,1,0:T(8,128)(2,1)}, f32[40,128]{1,0:T(8,128)}, f32[16,128]{1,0:T(8,128)}, f32[8,128]{1,0:T(8,128)}) custom-call(bf16[24,3072]{1,0:T(8,128)(2,1)} %images.1, s32[1,24]{1,0:T(1,128)} %bitcast.47, s32[1,24]{1,0:T(1,128)} %bitcast.48, s32[1,24]{1,0:T(1,128)} %bitcast.49, s32[4,8]{1,0:T(4,128)} %sizes.1, f32[16,27]{1,0:T(8,128)} %refs_3_.1, ...), custom_call_target="tpu_custom_call" | custom-call | tf_op jit(solution)/shard_map/pallas_call | solution.py:1011
  225.0 10.0 %shard_map.375 = (f32[2,3,240,640]{3,2,1,0:T(8,128)}, f32[2,3,240,640]{3,2,1,0:T(8,128)}, f32[2,3,240,640]{3,2,1,0:T(8,128)}, f32[16,27]{1,0:T(8,128)}, f32[16,2...) custom-call(bf16[2,3,256,640]{3,2,1,0:T(8,128)(2,1)} %get-tuple-elem, ...), custom_call_target="tpu_custom_call" | custom-call | tf_op jit(solution)/shard_map/pallas_call | solution.py:1103
